TPU v7x, 128 devices: a whole 4x4x4 slice. The times are simulated.
128 devices in a mesh: expert: 32 (over z, x, core), replica: 4 (over y).
Axes of the slice: x: 4, y: 4, z: 4, core: 2. Of those that a mesh axis runs over, the one named last changes fastest.
Arguments:
- grad_out: bfloat16 [16384, 2048], P(('expert', 'replica')), may hold values from -6 to 6
- gates: bfloat16 [16384, 8], P(('expert', 'replica')), may hold values from 0.019897461 to 0.5
- experts: int32 [16384, 8], P(('expert', 'replica')), may hold values from 0 to 127, all different within a row; in each aligned block of 128 rows (0 to 127, 128 to 255, ...) at most 20 rows name the same one
- hidden: bfloat16 [128, 4, 640, 768], P('expert', 'replica'), may hold values from -6 to 6
- down_weight: bfloat16 [2048, 128, 768], P(None, 'expert'), may hold values from -0.21875 to 0.21875
Outputs:
- d_hidden: bfloat16 [128, 4, 640, 768], P('expert', 'replica')
- d_down: bfloat16 [2048, 128, 768], P('replica', 'expert')
- d_gates: float32 [16384, 8], P(('expert', 'replica'))
Inputs may be any that keep to these rules, and one draw needn't show every extreme that they name: Each token names 8 different experts. Among the 128 tokens of one device no expert is named by more than 20 tokens, a bound that some block reaches.
All inputs are finite; a program needn't handle non-finite values.
Results may differ from a plain program's by a relative error of at most 0.013.
Values may be sent and summed in bfloat16 or wider, within the bound.
A program may use at most 192 MiB of HBM per device.

v0:
```python
import jax
import jax.numpy as jnp
from jax import lax
from jax.sharding import PartitionSpec as P

N_CHUNKS = 2


def per_device(grad_out, gates, experts, hidden, down_weight):
    expert_count = lax.axis_size("expert")
    replica_count = lax.axis_size("replica")
    me = lax.axis_index("expert")
    tok_rows = grad_out.shape[0]
    width = grad_out.shape[1]
    top_count = experts.shape[1]
    local_experts = hidden.shape[0]
    slot_count = hidden.shape[2]
    hidden_width = hidden.shape[3]
    capacity = slot_count // expert_count
    all_experts = local_experts * expert_count

    flat_ids = experts.reshape(-1)
    expert_range = jnp.arange(all_experts, dtype=jnp.int32)
    onehot_ids = (flat_ids[:, None] == expert_range[None, :]).astype(jnp.int32)
    running = jnp.cumsum(onehot_ids, axis=0)
    position = jnp.sum(onehot_ids * running, axis=1) - 1
    slot_index = (
        flat_ids % local_experts * expert_count + flat_ids // local_experts
    ) * capacity + position
    slot_index = slot_index.reshape(tok_rows, top_count)

    extra = 128
    info = jnp.concatenate(
        [
            grad_out,
            experts.astype(jnp.bfloat16),
            gates,
            jnp.zeros((tok_rows, extra - 2 * top_count), jnp.bfloat16),
        ],
        axis=1,
    )
    gathered = lax.all_gather(info, "expert")
    all_ids = gathered[:, :, width:width + top_count].astype(jnp.int32)
    all_gates = gathered[:, :, width + top_count:width + 2 * top_count].astype(jnp.float32)
    pair_ids = all_ids.reshape(expert_count, tok_rows * top_count).T
    local_ids = pair_ids - me * local_experts
    mine = local_ids[:, :, None] == jnp.arange(local_experts, dtype=jnp.int32)[None, None, :]
    mine = mine.reshape(tok_rows * top_count, expert_count * local_experts).astype(jnp.int32)
    rank = jnp.cumsum(mine, axis=0) - 1
    rank = jnp.where(mine > 0, rank, -1).reshape(tok_rows, top_count, expert_count, local_experts)
    owns = rank[..., None] == jnp.arange(capacity, dtype=jnp.int32)
    select = jnp.any(owns, axis=1)
    select = jnp.transpose(select, (1, 2, 3, 0)).reshape(
        expert_count, local_experts * capacity, tok_rows
    ).astype(jnp.bfloat16)
    gate_t = jnp.transpose(all_gates, (1, 2, 0))
    gate_slots = jnp.sum(
        jnp.where(owns, gate_t[:, :, :, None, None], 0.0), axis=(0, 1)
    )
    gate_slots = jnp.transpose(gate_slots, (1, 0, 2)).reshape(local_experts, slot_count)

    picked = jnp.einsum(
        "sqt,std->sqd", select, gathered, preferred_element_type=jnp.float32
    ).astype(jnp.bfloat16)
    picked = picked.reshape(expert_count, local_experts, capacity, width + extra)[:, :, :, :width]
    grad_slots = jnp.transpose(picked, (1, 0, 2, 3)).reshape(local_experts, slot_count, width)

    hidden_slots = hidden.reshape(local_experts, slot_count, hidden_width)
    weighted = (gate_slots[:, :, None] * hidden_slots.astype(jnp.float32)).astype(jnp.bfloat16)

    piece = width // (replica_count * N_CHUNKS)
    parts = grad_slots.reshape(local_experts, slot_count, replica_count, N_CHUNKS, piece)
    down_parts = []
    for c in range(N_CHUNKS):
        chunk = parts[:, :, :, c, :].reshape(local_experts, slot_count, replica_count * piece)
        down_parts.append(
            lax.psum_scatter(
                jnp.einsum(
                    "esd,esf->def", chunk, weighted, preferred_element_type=jnp.float32
                ).astype(jnp.bfloat16),
                "replica",
                scatter_dimension=0,
                tiled=True,
            )
        )
    down_grad = jnp.concatenate(down_parts, axis=0)
    upstream = jnp.einsum(
        "esd,def->esf", grad_slots, down_weight, preferred_element_type=jnp.float32
    )
    hidden_grad = (gate_slots[:, :, None] * upstream).astype(jnp.bfloat16).reshape(hidden.shape)
    slot_grad = jnp.sum(hidden_slots.astype(jnp.float32) * upstream, axis=2)
    returned = lax.all_to_all(
        slot_grad.reshape(local_experts, expert_count, capacity),
        "expert",
        split_axis=1,
        concat_axis=1,
        tiled=True,
    )
    gate_grad = jnp.take(returned.reshape(-1), slot_index, axis=0)
    return (hidden_grad, down_grad, gate_grad)


def solution(mesh):
    in_specs = (
        P(("expert", "replica"), None),
        P(("expert", "replica"), None),
        P(("expert", "replica"), None),
        P("expert", "replica", None, None),
        P(None, "expert", None),
    )
    out_specs = (
        P("expert", "replica", None, None),
        P("replica", "expert", None),
        P(("expert", "replica"), None),
    )
    return jax.shard_map(
        per_device, mesh=mesh, in_specs=in_specs, out_specs=out_specs, check_vma=False
    )
```

profile of v0, /device:TPU:1, one launch (start us, length us, event | category | flops | bytes accessed | tf_op | source)
XLA Modules:
  0.0 389.2 jit_solution(15496024720724847848)
XLA Ops:
  7.2 0.7 convert_element_type.44
  7.9 0.1 copy.160
  8.0 0.8 copy.161
  8.8 1.9 concatenate.6
  10.9 78.7 %all-gather.3.cloned.1.call-done = bf16[4096,2176]{1,0:T(8,128)(2,1)} async-done(((bf16[128,2176]{1,0:T(8,128)(2,1)}), bf16[4096,2176]{1,0:T(8,128)(2,1)}) %all-gather.3.cloned.1.call-update) | async-done | bytes 17825808 | tf_op jit(solution)/shard_map/all_gather | solution.py:42
  89.6 2.1 convert_bitcast_fusion.2
  91.7 0.6 copy.170
  92.3 0.3 copy.201
  92.7 0.2 copy.163
  92.9 0.2 copy.164
  93.1 0.1 eq.62
  93.2 0.2 eq.63
  93.4 0.1 convert_bitcast_fusion.3
  93.6 0.2 copy.165
  93.8 0.3 fusion.19
  94.2 0.1 copy.167
  94.3 0.2 copy.168
  94.6 6.5 %eq.68 = s32[128,8,32,4]{1,0,3,2:T(8,128)} reshape(s32[1024,128]{0,1:T(8,128)S(1)} %bitcast_select_fusion.1) | data formatting | bytes 1048576 | tf_op jit(solution)/shard_map/eq | solution.py:51
  101.1 5.2 %copy.169 = s32[128,8,32,4]{0,2,3,1:T(8,128)S(1)} copy(s32[128,8,32,4]{1,0,3,2:T(8,128)} %eq.68) | data formatting | bytes 1048576 | tf_op jit(solution)/shard_map/eq | solution.py:51
  106.2 1.7 fusion.3
  107.9 1.1 select_reduce_fusion
  109.1 0.1 mul.40
  109.2 10.2 %convolution_convert_fusion = bf16[32,80,2176]{2,1,0:T(8,128)(2,1)} fusion(bf16[32,128,2176]{2,1,0:T(8,128)(2,1)} %bitcast.57, pred[32,80,128]{2,0,1:T(8,128)(4,1)S(1)} %bitcast.60), kind=kOutput, calls=%fused_computation.12 | convolution fusion | flops 1431633920 | bytes 29294592 | tf_op jit(solution)/shard_map/sqt,std->sqd/dot_general | solution.py:62
  119.4 12.1 %copy.173 = bf16[32,80,2176]{2,0,1:T(8,128)(2,1)} copy(bf16[32,80,2176]{2,1,0:T(8,128)(2,1)} %convolution_convert_fusion) | data formatting | bytes 22282240 | tf_op jit(solution)/shard_map/convert_element_type | solution.py:64
  131.6 10.0 %slice_bitcast_fusion = bf16[4,32,20,2048]{3,1,2,0:T(8,128)(2,1)} fusion(bf16[32,4,20,2176]{3,0,2,1:T(8,128)(2,1)} %bitcast.58), kind=kLoop, calls=%fused_computation.5 | loop fusion | bytes 20971520 | tf_op jit(solution)/shard_map/transpose | solution.py:66
  141.6 14.7 %copy.174 = bf16[4,32,20,2048]{3,0,2,1:T(4,128)(2,1)} copy(bf16[4,32,20,2048]{3,1,2,0:T(8,128)(2,1)} %slice_bitcast_fusion) | data formatting | bytes 20971520 | tf_op jit(solution)/shard_map/transpose | solution.py:66
  156.3 17.8 %reshape_reshape.3 = bf16[4,640,4,2,256]{4,3,2,0,1:T(2,128)(2,1)} reshape(bf16[4,32,20,2048]{3,0,2,1:T(4,128)(2,1)} %copy.174) | data formatting | bytes 20971520 | tf_op jit(solution)/shard_map/reshape;reshape | solution.py:72
  174.1 53.7 %slice_reduce_fusion.1 = (bf16[4,640,4,256]{3,2,0,1:T(4,128)(2,1)}, bf16[4,640,4,256]{3,2,0,1:T(4,128)(2,1)}) fusion(bf16[4,640,4,2,256]{4,3,2,0,1:T(2,128)(2,1)} %reshape_reshape.3), kind=kLoop, calls=%fused_computation.4 | loop fusion | bytes 20971520 | tf_op jit(solution)/shard_map/slice | solution.py:75
  227.8 8.7 %reshape.98 = bf16[4,640,1024]{2,0,1:T(4,128)(2,1)} reshape(bf16[4,640,4,256]{3,2,0,1:T(4,128)(2,1)} %get-tuple-element.22) | data formatting | bytes 10485760 | tf_op jit(solution)/shard_map/reshape;squeeze | solution.py:75
  236.5 10.9 %convert_bitcast_fusion = bf16[1024,4,768]{0,2,1:T(8,128)(2,1)} fusion(bf16[4,640,1024]{2,0,1:T(4,128)(2,1)} %reshape.98, bf16[4,1,640,768]{3,2,1,0:T(8,128)(2,1)} %param.8, f32[4,640]{1,0:T(4,128)S(1)} %mul.40), kind=kOutput, calls=%fused_computation.16 | convolution fusion | flops 4035575808 | bytes 15476736 | tf_op jit(solution)/shard_map/esd,esf->def/dot_general | solution.py:78
  247.5 8.8 %reshape.97 = bf16[4,640,1024]{2,0,1:T(4,128)(2,1)} reshape(bf16[4,640,4,256]{3,2,0,1:T(4,128)(2,1)} %get-tuple-element.21) | data formatting | bytes 10485760 | tf_op jit(solution)/shard_map/reshape;squeeze | solution.py:75
  256.3 11.1 %convert_bitcast_fusion.1 = bf16[1024,4,768]{0,2,1:T(8,128)(2,1)} fusion(bf16[4,640,1024]{2,0,1:T(4,128)(2,1)} %reshape.97, bf16[4,1,640,768]{3,2,1,0:T(8,128)(2,1)} %param.8, f32[4,640]{1,0:T(4,128)S(1)} %mul.40), kind=kOutput, calls=%fused_computation.17 | convolution fusion | flops 4035575808 | bytes 15476736 | tf_op jit(solution)/shard_map/esd,esf->def/dot_general | solution.py:78
  267.4 0.1 copy.183
  267.7 0.1 copy.189
  267.8 0.2 fusion.21
  268.1 0.1 copy.190
  268.2 0.2 copy.191
  268.8 35.4 %fusion.5 = (f32[4,640]{1,0:T(4,128)S(1)}, bf16[4,1,640,768]{3,2,1,0:T(8,128)(2,1)}) fusion(bf16[4,1,640,768]{3,2,1,0:T(8,128)(2,1)} %param.8, f32[4,640]{1,0:T(4,128)S(1)} %mul.40, bf16[2048,4,768]{2,1,0:T(4,128)(2,1)} %param.9, bf16[4,640,2048]{2,0,1:T(4,128)(2,1)} %bitcast.59), kind=kOutput, calls=%fused_computation.14 | convolution fusion | flops 8062891520 | bytes 30953472 | tf_op jit(solution)/shard_map/esd,def->esf/dot_general | solution.py:87
  304.1 0.1 reshape.83
  304.2 0.7 copy.192
  304.9 6.3 %all-to-all-start = ((f32[4,32,20]{2,0,1:T(4,128)}), f32[4,32,20]{2,0,1:T(4,128)S(1)}, u32[]{:S(2)}, u32[]{:S(2)}) async-start(f32[4,32,20]{2,0,1:T(4,128)} %copy.192), calls=%async_computation.2 | async-start | bytes 131072 | tf_op jit(solution)/shard_map/all_to_all | solution.py:92
  311.3 7.3 %all-to-all-done = f32[4,32,20]{2,0,1:T(4,128)S(1)} async-done(((f32[4,32,20]{2,0,1:T(4,128)}), f32[4,32,20]{2,0,1:T(4,128)S(1)}, u32[]{:S(2)}, u32[]{:S(2)}) %all-to-all-start) | async-done | bytes 10272 | tf_op jit(solution)/shard_map/all_to_all | solution.py:92
  318.6 0.1 reshape.84
  318.7 6.2 %gather_fusion = f32[1024]{0:T(1024)S(1)} fusion(f32[2560]{0:T(1024)S(1)} %reshape.84, s32[1024]{0:T(1024)S(1)} %broadcast_clamp_fusion), kind=kCustom, calls=%fused_computation | custom fusion | bytes 12288 | tf_op jit(solution)/shard_map/jit(_take)/gather | solution.py:99
  325.0 0.7 copy.196
  325.6 51.1 %reduce-scatter.3.cloned.1.call-done = bf16[256,4,768]{0,2,1:T(8,128)(2,1)} async-done(((bf16[1024,4,768]{0,2,1:T(8,128)(2,1)}), bf16[256,4,768]{0,2,1:T(8,128)(2,1)}) %reduce-scatter.3.cloned.1.call-update) | async-done | bytes 1572880 | tf_op jit(solution)/shard_map/reduce_scatter | solution.py:77
  376.8 2.1 pad_maximum_fusion
  378.9 3.6 copy.195
  (34 shorter events, 1.2 us)
Async XLA Ops:
  7.2 82.4 %all-gather.3.cloned.1.call-start = ((), (), s32[]{:S(2)}) async-start(), calls=%async_computation.5 | async-start | bytes 18382848 | tf_op jit(solution)/shard_map/all_gather | solution.py:42
  10.7 314.9 %reduce-scatter.5.cloned.1.call-start = ((), (), s32[]{:S(2)}) async-start(), calls=%async_computation.4 | async-start | bytes 7864320 | tf_op jit(solution)/shard_map/reduce_scatter | solution.py:77
  247.5 129.3 %reduce-scatter.3.cloned.1.call-start = ((), (), s32[]{:S(2)}) async-start(), calls=%async_computation.3 | async-start | bytes 7864320 | tf_op jit(solution)/shard_map/reduce_scatter | solution.py:77
  256.3 11.1 %copy-start = (s32[128,8]{0,1:T(8,128)S(1)}, s32[128,8]{0,1:T(8,128)}, u32[]{:S(2)}) copy-start(s32[128,8]{0,1:T(8,128)} %param.7) | copy-start | bytes 12292
  304.9 13.7 %all-to-all-start = ((f32[4,32,20]{2,0,1:T(4,128)}), f32[4,32,20]{2,0,1:T(4,128)S(1)}, u32[]{:S(2)}, u32[]{:S(2)}) async-start(f32[4,32,20]{2,0,1:T(4,128)} %copy.192), calls=%async_computation.2 | async-start | bytes 131072 | tf_op jit(solution)/shard_map/all_to_all | solution.py:92
Sparse Core Ops, SparseCore 0:
  10.8 78.6 all-gather.2
  247.6 62.9 reduce-scatter.4
  313.0 63.6 reduce-scatter.2
where the time goes:
time: 393 us; the launch traced here: 389 us
  local copies, waits for them, and re-layouts  155 us (39%)
  waiting for transfers between devices  137 us (35%)
  matrix products  67.5 us (17%)
  between operations  14.3 us (4%)
  other arithmetic  8.78 us (2%)
  starting transfers between devices  6.47 us (2%)
    all_gather x1, waiting for transfers between devices, per_device(): gathered = lax.all_gather(info, 'expert')  78.7 us
    slice x1, local copies, waits for them, and re-layouts, per_device(): parts[:, :, :, c, :]  53.7 us
    reduce_scatter x2, waiting for transfers between devices, per_device(): lax.psum_scatter(jnp.einsum('esd,esf->def', chunk, weighted, preferred_el...  51.1 us
    dot_general x1, matrix products, per_device(): jnp.einsum('esd,def->esf', grad_slots, down_weight, preferred_element_typ...  35.4 us
    transpose x2, local copies, waits for them, and re-layouts, per_device(): jnp.transpose(picked, (1, 0, 2, 3))  24.8 us
    dot_general x2, matrix products, per_device(): jnp.einsum('esd,esf->def', chunk, weighted, preferred_element_type=jnp.fl...  22 us
    another operation x1, local copies, waits for them, and re-layouts, per_device(): grad_slots.reshape(local_experts, slot_count, replica_count, N_CHUNKS, pi...  17.8 us
    another operation x2, local copies, waits for them, and re-layouts, per_device(): parts[:, :, :, c, :]  17.5 us
  transfers between devices with their start and end apart: 4, of which 3 were waited for; matrix products, arithmetic and copies ran while one was open for 17% of the time, Pallas kernels for 0%

commit v1 on v0

--- a/solution.py
+++ b/solution.py
@@ -2,8 +2,6 @@
 import jax.numpy as jnp
 from jax import lax
 from jax.sharding import PartitionSpec as P
-
-N_CHUNKS = 2
 
 
 def per_device(grad_out, gates, experts, hidden, down_weight):
@@ -50,40 +48,37 @@
     rank = jnp.where(mine > 0, rank, -1).reshape(tok_rows, top_count, expert_count, local_experts)
     owns = rank[..., None] == jnp.arange(capacity, dtype=jnp.int32)
     select = jnp.any(owns, axis=1)
-    select = jnp.transpose(select, (1, 2, 3, 0)).reshape(
-        expert_count, local_experts * capacity, tok_rows
-    ).astype(jnp.bfloat16)
     gate_t = jnp.transpose(all_gates, (1, 2, 0))
     gate_slots = jnp.sum(
         jnp.where(owns, gate_t[:, :, :, None, None], 0.0), axis=(0, 1)
     )
     gate_slots = jnp.transpose(gate_slots, (1, 0, 2)).reshape(local_experts, slot_count)
 
-    picked = jnp.einsum(
-        "sqt,std->sqd", select, gathered, preferred_element_type=jnp.float32
-    ).astype(jnp.bfloat16)
-    picked = picked.reshape(expert_count, local_experts, capacity, width + extra)[:, :, :, :width]
-    grad_slots = jnp.transpose(picked, (1, 0, 2, 3)).reshape(local_experts, slot_count, width)
+    group = 4
+    groups = expert_count // group
+    select = jnp.transpose(select, (2, 1, 3, 0)).reshape(
+        local_experts, groups, group, capacity, 1, tok_rows
+    )
+    diagonal = jnp.eye(group, dtype=jnp.bool_).reshape(1, 1, group, 1, group, 1)
+    blocks = jnp.logical_and(select, diagonal).astype(jnp.bfloat16).reshape(
+        local_experts, groups, group * capacity, group * tok_rows
+    )
+    rows_of = gathered[:, :, :width].reshape(groups, group * tok_rows, width)
+    grad_slots = jnp.einsum(
+        "jgqu,gud->jgqd", blocks, rows_of, preferred_element_type=jnp.float32
+    ).astype(jnp.bfloat16).reshape(local_experts, slot_count, width)
 
     hidden_slots = hidden.reshape(local_experts, slot_count, hidden_width)
     weighted = (gate_slots[:, :, None] * hidden_slots.astype(jnp.float32)).astype(jnp.bfloat16)
 
-    piece = width // (replica_count * N_CHUNKS)
-    parts = grad_slots.reshape(local_experts, slot_count, replica_count, N_CHUNKS, piece)
-    down_parts = []
-    for c in range(N_CHUNKS):
-        chunk = parts[:, :, :, c, :].reshape(local_experts, slot_count, replica_count * piece)
-        down_parts.append(
-            lax.psum_scatter(
-                jnp.einsum(
-                    "esd,esf->def", chunk, weighted, preferred_element_type=jnp.float32
-                ).astype(jnp.bfloat16),
-                "replica",
-                scatter_dimension=0,
-                tiled=True,
-            )
-        )
-    down_grad = jnp.concatenate(down_parts, axis=0)
+    down_grad = lax.psum_scatter(
+        jnp.einsum(
+            "esd,esf->def", grad_slots, weighted, preferred_element_type=jnp.float32
+        ).astype(jnp.bfloat16),
+        "replica",
+        scatter_dimension=0,
+        tiled=True,
+    )
     upstream = jnp.einsum(
         "esd,def->esf", grad_slots, down_weight, preferred_element_type=jnp.float32
     )

time: 393 us -> 292 us (0.74)
  local copies, waits for them, and re-layouts: 155 us -> 59.5 us
  waiting for transfers between devices: 137 us -> 158 us
  matrix products: 67.5 us -> 48.3 us
    slice x1, local copies, waits for them, and re-layouts: 53.7 us -> 14.1 us  [per_device(): rows_of = gathered[:, :, :width].reshape(groups, group * tok_rows, width)]
    another operation x9 -> x6, local copies, waits for them, and re-layouts: 35.6 us -> 0.31 us  [the longest x1 17.8 us: per_device(): grad_slots.reshape(local_experts, slot_count, replica_count, N_CHUNKS, pi...]
    transpose x3 -> x1, local copies, waits for them, and re-layouts: 25 us -> 0.19 us  [the longest x2 24.8 us: per_device(): jnp.transpose(picked, (1, 0, 2, 3))]
    reduce_scatter x2 -> x1, waiting for transfers between devices: 51.1 us -> 71.7 us  [per_device(): lax.psum_scatter(jnp.einsum('esd,esf->def', grad_slots, weighted, preferr...]
    dot_general x1, matrix products: 35.4 us -> 20 us  [per_device(): jnp.einsum('esd,def->esf', grad_slots, down_weight, preferred_element_typ...]
    dot_general x3 -> x2, matrix products: 32.2 us -> 28.3 us  [the longest x1 16.8 us: per_device(): jnp.einsum('esd,esf->def', grad_slots, weighted, preferred_element_type=j...]
    unnamed x7 -> x8, local copies, waits for them, and re-layouts: 5.5 us -> 9.34 us
  transfers between devices with their start and end apart: 4 -> 3, of which waited for: 3 -> 3; matrix products, arithmetic and copies ran while one was open for 17% -> 10% of each run, Pallas kernels for 0% -> 0%
where the time goes in v1:
time: 292 us; the launch traced here: 291 us
  waiting for transfers between devices  158 us (54%)
  local copies, waits for them, and re-layouts  59.5 us (20%)
  matrix products  48.3 us (17%)
  between operations  14.3 us (5%)
  other arithmetic  6.73 us (2%)
  starting transfers between devices  4.89 us (2%)
    all_gather x1, waiting for transfers between devices, per_device(): gathered = lax.all_gather(info, 'expert')  78.5 us
    reduce_scatter x1, waiting for transfers between devices, per_device(): lax.psum_scatter(jnp.einsum('esd,esf->def', grad_slots, weighted, preferr...  71.7 us
    dot_general x1, matrix products, per_device(): jnp.einsum('esd,def->esf', grad_slots, down_weight, preferred_element_typ...  20 us
    dot_general x1, matrix products, per_device(): jnp.einsum('esd,esf->def', grad_slots, weighted, preferred_element_type=j...  16.8 us
    slice x1, local copies, waits for them, and re-layouts, per_device(): rows_of = gathered[:, :, :width].reshape(groups, group * tok_rows, width)  14.1 us
    dot_general x1, matrix products, per_device(): jnp.einsum('jgqu,gud->jgqd', blocks, rows_of, preferred_element_type=jnp....  11.5 us
    eq x2, local copies, waits for them, and re-layouts, per_device(): owns = rank[..., None] == jnp.arange(capacity, dtype=jnp.int32)  11.3 us
    convert_element_type x1, local copies, waits for them, and re-layouts, per_device(): grad_slots = jnp.einsum('jgqu,gud->jgqd', blocks, rows_of, preferred_elem...  10.1 us
  transfers between devices with their start and end apart: 3, of which 3 were waited for; matrix products, arithmetic and copies ran while one was open for 10% of the time, Pallas kernels for 0%

profile of v1, /device:TPU:1, one launch (start us, length us, event | category | flops | bytes accessed | tf_op | source)
XLA Modules:
  0.0 291.3 jit_solution(12314243346861585460)
XLA Ops:
  7.2 0.7 convert_element_type.41
  7.9 0.1 copy.73
  8.0 0.8 copy.74
  8.8 1.9 concatenate.3
  10.8 0.1 eq.72
  10.9 0.1 and.44
  11.0 78.5 %all-gather.3.cloned.1.call-done = bf16[4096,2176]{1,0:T(8,128)(2,1)} async-done(((bf16[128,2176]{1,0:T(8,128)(2,1)}), bf16[4096,2176]{1,0:T(8,128)(2,1)}) %all-gather.3.cloned.1.call-update) | async-done | bytes 17825808 | tf_op jit(solution)/shard_map/all_gather | solution.py:40
  89.6 2.1 convert_bitcast_fusion.2
  91.7 14.1 %slice.34 = bf16[32,128,2048]{2,1,0:T(8,128)(2,1)} slice(bf16[32,128,2176]{2,1,0:T(8,128)(2,1)} %bitcast.64), slice={[0:32], [0:128], [0:2048]} | slice | bytes 33554432 | tf_op jit(solution)/shard_map/slice | solution.py:66
  105.8 0.6 copy.82
  106.4 1.1 copy.105
  107.6 0.2 copy.76
  107.8 0.1 eq.69
  107.9 0.2 eq.70
  108.1 0.1 convert_bitcast_fusion.3
  108.3 0.2 copy.77
  108.5 0.3 fusion.12
  108.9 0.1 copy.79
  109.0 0.2 copy.80
  109.2 6.2 %eq.75 = s32[128,8,32,4]{1,0,3,2:T(8,128)} reshape(s32[1024,128]{0,1:T(8,128)S(1)} %bitcast_select_fusion.1) | data formatting | bytes 1048576 | tf_op jit(solution)/shard_map/eq | solution.py:49
  115.4 5.2 %copy.81 = s32[128,8,32,4]{0,2,3,1:T(8,128)S(1)} copy(s32[128,8,32,4]{1,0,3,2:T(8,128)} %eq.75) | data formatting | bytes 1048576 | tf_op jit(solution)/shard_map/eq | solution.py:49
  120.6 1.7 fusion.2
  122.3 1.1 select_reduce_fusion
  123.4 0.1 copy.83
  123.5 0.1 mul.40
  123.6 0.2 copy.84
  123.8 1.4 and.42
  125.2 1.2 and.43
  126.4 11.5 %convert_bitcast_fusion.1 = bf16[4,8,80,2048]{3,2,0,1:T(8,128)(2,1)} fusion(bf16[8,512,2048,1]{2,1,3,0:T(8,128)(2,1)} %bitcast.65, pred[4,8,80,512]{3,2,0,1:T(8,128)(4,1)S(1)} %and.43, pred[80,512]{1,0:T(8,128)(4,1)S(1)} %bitcast.74), kind=kOutput, calls=%fused_computation.4 | convolution fusion | flops 5375262720 | bytes 28614656 | tf_op jit(solution)/shard_map/jgqu,gud->jgqd/dot_general | solution.py:67
  137.9 10.1 %copy.85 = bf16[4,8,80,2048]{3,2,1,0:T(8,128)(2,1)} copy(bf16[4,8,80,2048]{3,2,0,1:T(8,128)(2,1)} %convert_bitcast_fusion.1) | data formatting | bytes 20971520 | tf_op jit(solution)/shard_map/convert_element_type | solution.py:69
  148.0 16.8 %convert_bitcast_fusion = bf16[2048,4,768]{0,2,1:T(8,128)(2,1)} fusion(bf16[4,640,2048]{2,1,0:T(8,128)(2,1)} %bitcast.66, bf16[4,1,640,768]{3,2,1,0:T(8,128)(2,1)} %param.8, f32[4,640]{1,0:T(4,128)S(1)} %mul.40), kind=kOutput, calls=%fused_computation.3 | convolution fusion | flops 8065253376 | bytes 27011072 | tf_op jit(solution)/shard_map/esd,esf->def/dot_general | solution.py:75
  164.8 0.7 copy-done
  165.5 0.1 copy.89
  165.6 0.1 eq.84
  165.8 0.1 copy.95
  165.9 0.2 fusion.14
  166.2 0.1 copy.96
  166.3 0.2 copy.97
  166.9 20.0 %fusion.4 = (f32[4,640]{1,0:T(4,128)S(1)}, bf16[4,1,640,768]{3,2,1,0:T(8,128)(2,1)}) fusion(bf16[4,1,640,768]{3,2,1,0:T(8,128)(2,1)} %param.8, f32[4,640]{1,0:T(4,128)S(1)} %mul.40, bf16[4,640,2048]{2,1,0:T(8,128)(2,1)} %bitcast.67, bf16[2048,4,768]{2,1,0:T(4,128)(2,1)} %param.9), kind=kOutput, calls=%fused_computation.11 | convolution fusion | flops 8062891520 | bytes 30953472 | tf_op jit(solution)/shard_map/esd,def->esf/dot_general | solution.py:82
  186.9 0.1 reshape.92
  187.0 0.7 copy.98
  187.7 4.8 %all-to-all-start = ((f32[4,32,20]{2,0,1:T(4,128)}), f32[4,32,20]{2,0,1:T(4,128)S(1)}, u32[]{:S(2)}, u32[]{:S(2)}) async-start(f32[4,32,20]{2,0,1:T(4,128)} %copy.98), calls=%async_computation.1 | async-start | bytes 131072 | tf_op jit(solution)/shard_map/all_to_all | solution.py:87
  192.5 7.3 %all-to-all-done = f32[4,32,20]{2,0,1:T(4,128)S(1)} async-done(((f32[4,32,20]{2,0,1:T(4,128)}), f32[4,32,20]{2,0,1:T(4,128)S(1)}, u32[]{:S(2)}, u32[]{:S(2)}) %all-to-all-start) | async-done | bytes 10272 | tf_op jit(solution)/shard_map/all_to_all | solution.py:87
  199.8 0.1 reshape.93
  199.9 6.2 %gather_fusion = f32[1024]{0:T(1024)S(1)} fusion(f32[2560]{0:T(1024)S(1)} %reshape.93, s32[1024]{0:T(1024)S(1)} %broadcast_clamp_fusion), kind=kCustom, calls=%fused_computation | custom fusion | bytes 12288 | tf_op jit(solution)/shard_map/jit(_take)/gather | solution.py:94
  206.2 0.7 copy.102
  206.8 71.7 %reduce-scatter.2.cloned.1.call-done = bf16[512,4,768]{0,2,1:T(8,128)(2,1)} async-done(((bf16[2048,4,768]{0,2,1:T(8,128)(2,1)}), bf16[512,4,768]{0,2,1:T(8,128)(2,1)}) %reduce-scatter.2.cloned.1.call-update) | async-done | bytes 3145744 | tf_op jit(solution)/shard_map/reduce_scatter | solution.py:74
  278.5 6.0 %copy.101 = bf16[512,4,768]{2,1,0:T(4,128)(2,1)} copy(bf16[512,4,768]{0,2,1:T(8,128)(2,1)} %reduce-scatter.2.cloned.1.call-done) | data formatting | bytes 6291456
  (29 shorter events, 1.0 us)
Async XLA Ops:
  7.2 82.4 %all-gather.3.cloned.1.call-start = ((), (), s32[]{:S(2)}) async-start(), calls=%async_computation.3 | async-start | bytes 18382848 | tf_op jit(solution)/shard_map/all_gather | solution.py:40
  10.7 267.8 %reduce-scatter.2.cloned.1.call-start = ((), (), s32[]{:S(2)}) async-start(), calls=%async_computation.2 | async-start | bytes 15728640 | tf_op jit(solution)/shard_map/reduce_scatter | solution.py:74
  164.8 0.7 copy-start
  187.7 12.1 %all-to-all-start = ((f32[4,32,20]{2,0,1:T(4,128)}), f32[4,32,20]{2,0,1:T(4,128)S(1)}, u32[]{:S(2)}, u32[]{:S(2)}) async-start(f32[4,32,20]{2,0,1:T(4,128)} %copy.98), calls=%async_computation.1 | async-start | bytes 131072 | tf_op jit(solution)/shard_map/all_to_all | solution.py:87
Sparse Core Ops, SparseCore 0:
  10.8 78.6 all-gather.2
  165.0 113.4 reduce-scatter.1

commit v2 on v1

--- a/solution.py
+++ b/solution.py
@@ -1,7 +1,41 @@
 import jax
 import jax.numpy as jnp
 from jax import lax
+from jax.experimental import pallas as pl
 from jax.sharding import PartitionSpec as P
+
+
+def pick_kernel(column_ref, rows_ref, out_ref):
+    column = column_ref[0, 0]
+    group, tok, width = rows_ref.shape
+    onehot = (
+        column == lax.broadcasted_iota(jnp.int32, (column.shape[0], group * tok), 1)
+    ).astype(rows_ref.dtype)
+    rows = rows_ref[...].reshape(group * tok, width)
+    out_ref[0, 0] = jnp.dot(onehot, rows, preferred_element_type=jnp.float32).astype(
+        out_ref.dtype
+    )
+
+
+def pick(column, gathered, width):
+    local_experts, groups, block, _ = column.shape
+    sources, tok, _ = gathered.shape
+    group = sources // groups
+    return pl.pallas_call(
+        pick_kernel,
+        out_shape=jax.ShapeDtypeStruct((local_experts, groups, block, width), gathered.dtype),
+        grid=(groups, local_experts),
+        in_specs=[
+            pl.BlockSpec((1, 1, block, 1), lambda g, j: (j, g, 0, 0)),
+            pl.BlockSpec((group, tok, width), lambda g, j: (g, 0, 0)),
+        ],
+        out_specs=pl.BlockSpec((1, 1, block, width), lambda g, j: (j, g, 0, 0)),
+        cost_estimate=pl.CostEstimate(
+            flops=2 * local_experts * groups * block * group * tok * width,
+            bytes_accessed=sources * tok * width * 2 + local_experts * groups * block * width * 2,
+            transcendentals=0,
+        ),
+    )(column, gathered)
 
 
 def per_device(grad_out, gates, experts, hidden, down_weight):
@@ -45,28 +79,24 @@
     mine = local_ids[:, :, None] == jnp.arange(local_experts, dtype=jnp.int32)[None, None, :]
     mine = mine.reshape(tok_rows * top_count, expert_count * local_experts).astype(jnp.int32)
     rank = jnp.cumsum(mine, axis=0) - 1
-    rank = jnp.where(mine > 0, rank, -1).reshape(tok_rows, top_count, expert_count, local_experts)
-    owns = rank[..., None] == jnp.arange(capacity, dtype=jnp.int32)
-    select = jnp.any(owns, axis=1)
-    gate_t = jnp.transpose(all_gates, (1, 2, 0))
-    gate_slots = jnp.sum(
-        jnp.where(owns, gate_t[:, :, :, None, None], 0.0), axis=(0, 1)
+    rank = jnp.where(mine > 0, rank, -1).reshape(
+        tok_rows * top_count, expert_count, local_experts
     )
+    hit = rank[..., None] == jnp.arange(capacity, dtype=jnp.int32)
+    token_of = (jnp.arange(tok_rows * top_count, dtype=jnp.int32) // top_count + 1)
+    owner = jnp.sum(jnp.where(hit, token_of[:, None, None, None], 0), axis=0) - 1
+    gate_pairs = all_gates.reshape(expert_count, tok_rows * top_count).T
+    gate_slots = jnp.sum(jnp.where(hit, gate_pairs[:, :, None, None], 0.0), axis=0)
     gate_slots = jnp.transpose(gate_slots, (1, 0, 2)).reshape(local_experts, slot_count)
 
     group = 4
     groups = expert_count // group
-    select = jnp.transpose(select, (2, 1, 3, 0)).reshape(
-        local_experts, groups, group, capacity, 1, tok_rows
+    within = (jnp.arange(expert_count, dtype=jnp.int32) % group * tok_rows)[:, None, None]
+    column = jnp.where(owner >= 0, owner + within, -1)
+    column = jnp.transpose(column, (1, 0, 2)).reshape(
+        local_experts, groups, group * capacity, 1
     )
-    diagonal = jnp.eye(group, dtype=jnp.bool_).reshape(1, 1, group, 1, group, 1)
-    blocks = jnp.logical_and(select, diagonal).astype(jnp.bfloat16).reshape(
-        local_experts, groups, group * capacity, group * tok_rows
-    )
-    rows_of = gathered[:, :, :width].reshape(groups, group * tok_rows, width)
-    grad_slots = jnp.einsum(
-        "jgqu,gud->jgqd", blocks, rows_of, preferred_element_type=jnp.float32
-    ).astype(jnp.bfloat16).reshape(local_experts, slot_count, width)
+    grad_slots = pick(column, gathered, width).reshape(local_experts, slot_count, width)
 
     hidden_slots = hidden.reshape(local_experts, slot_count, hidden_width)
     weighted = (gate_slots[:, :, None] * hidden_slots.astype(jnp.float32)).astype(jnp.bfloat16)

time: 292 us -> 278 us (0.952)
  local copies, waits for them, and re-layouts: 59.5 us -> 23.6 us
  Pallas kernels: 0 us -> 31 us
  matrix products: 48.3 us -> 36.3 us
    pallas_call x0 -> x1, Pallas kernels: none -> 31 us  [pick(): pl.pallas_call(pick_kernel, out_shape=jax.ShapeDtypeStruct((local_experts...]
    slice x1 -> x0, local copies, waits for them, and re-layouts: 14.1 us -> none  [per_device(): rows_of = gathered[:, :, :width].reshape(groups, group * tok_rows, width)]
    dot_general x1 -> x0, matrix products: 11.5 us -> none  [per_device(): jnp.einsum('jgqu,gud->jgqd', blocks, rows_of, preferred_element_type=jnp....]
    eq x2, local copies, waits for them, and re-layouts: 11.3 us -> 0.46 us  [per_device(): hit = rank[..., None] == jnp.arange(capacity, dtype=jnp.int32)]
    convert_element_type x1 -> x0, local copies, waits for them, and re-layouts: 10.1 us -> none  [per_device(): grad_slots = jnp.einsum('jgqu,gud->jgqd', blocks, rows_of, preferred_elem...]
    unnamed x8 -> x6, local copies, waits for them, and re-layouts: 9.34 us -> 8.18 us
where the time goes in v2:
time: 278 us; the launch traced here: 276 us
  waiting for transfers between devices  158 us (57%)
  matrix products  36.3 us (13%)
  Pallas kernels  31 us (11%)
  local copies, waits for them, and re-layouts  23.6 us (8%)
  between operations  14.3 us (5%)
  other arithmetic  7.39 us (3%)
  starting transfers between devices  5.18 us (2%)
    all_gather x1, waiting for transfers between devices, per_device(): gathered = lax.all_gather(info, 'expert')  78.7 us
    reduce_scatter x1, waiting for transfers between devices, per_device(): lax.psum_scatter(jnp.einsum('esd,esf->def', grad_slots, weighted, preferr...  71.9 us
    pallas_call x1, Pallas kernels, pick(): pl.pallas_call(pick_kernel, out_shape=jax.ShapeDtypeStruct((local_experts...  31 us
    dot_general x1, matrix products, per_device(): jnp.einsum('esd,def->esf', grad_slots, down_weight, preferred_element_typ...  19.6 us
    dot_general x1, matrix products, per_device(): jnp.einsum('esd,esf->def', grad_slots, weighted, preferred_element_type=j...  16.8 us
    unnamed x6, local copies, waits for them, and re-layouts  8.18 us
    all_to_all x1, waiting for transfers between devices, per_device(): lax.all_to_all(slot_grad.reshape(local_experts, expert_count, capacity),...  7.31 us
    gather x2, local copies, waits for them, and re-layouts, per_device(): gate_grad = jnp.take(returned.reshape(-1), slot_index, axis=0)  6.23 us
  transfers between devices with their start and end apart: 3, of which 3 were waited for; matrix products, arithmetic and copies ran while one was open for 10% of the time, Pallas kernels for 0%

profile of v2, /device:TPU:1, one launch (start us, length us, event | category | flops | bytes accessed | tf_op | source)
XLA Modules:
  0.0 275.7 jit_solution(6527785231494371038)
XLA Ops:
  7.2 0.7 convert_element_type.34
  7.9 0.1 copy.102
  8.0 0.8 copy.103
  8.8 1.9 concatenate.3
  10.8 0.1 eq.67
  10.9 78.7 %all-gather.3.cloned.1.call-done = bf16[4096,2176]{1,0:T(8,128)(2,1)} async-done(((bf16[128,2176]{1,0:T(8,128)(2,1)}), bf16[4096,2176]{1,0:T(8,128)(2,1)}) %all-gather.3.cloned.1.call-update) | async-done | bytes 17825808 | tf_op jit(solution)/shard_map/all_gather | solution.py:74
  89.6 1.6 slice_convert_fusion
  91.2 1.0 copy.111
  92.2 0.2 copy.112
  92.4 1.5 convert_subtract_fusion
  93.9 1.0 copy.104
  94.9 0.2 copy.105
  95.1 0.1 eq.64
  95.3 0.2 eq.65
  95.5 0.1 convert_bitcast_fusion.1
  95.6 0.2 copy.106
  95.8 0.3 fusion.9
  96.2 0.1 copy.108
  96.3 0.2 copy.109
  96.6 0.1 eq.70
  96.7 0.3 copy.110
  97.1 1.1 select_reduce_fusion.1
  98.2 0.1 copy.113
  98.3 0.1 mul.50
  98.4 1.5 select_reduce_fusion
  99.8 0.1 copy.114
  99.9 1.5 reshape.123.column_ref
  101.4 31.0 %shard_map.76 = bf16[4,8,80,2048]{3,2,1,0:T(8,128)(2,1)} custom-call(s32[4,8,80,1]{3,2,1,0:T(8,128)} %reshape.123.column_ref, bf16[32,128,2176]{2,1,0:T(8,128)(2,1)} %bitcast.49), custom_call_target="tpu_custom_call" | custom-call | flops 5368709120 | bytes 27262976 | tf_op jit(solution)/shard_map/pallas_call | solution.py:24
  132.4 16.8 %convert_bitcast_fusion = bf16[2048,4,768]{0,2,1:T(8,128)(2,1)} fusion(bf16[4,640,2048]{2,1,0:T(8,128)(2,1)} %bitcast.50, bf16[4,1,640,768]{3,2,1,0:T(8,128)(2,1)} %param.8, f32[4,640]{1,0:T(4,128)S(1)} %mul.50), kind=kOutput, calls=%fused_computation.3 | convolution fusion | flops 8065253376 | bytes 27011072 | tf_op jit(solution)/shard_map/esd,esf->def/dot_general | solution.py:105
  149.2 0.7 copy-done
  149.9 0.1 copy.119
  150.0 0.1 eq.78
  150.1 0.1 eq.74
  150.2 0.1 copy.125
  150.3 0.2 fusion.11
  150.6 0.1 copy.126
  150.7 0.2 copy.127
  151.1 0.1 reshape.114
  151.2 19.6 %fusion.3 = (f32[4,640]{1,0:T(4,128)S(1)}, bf16[4,1,640,768]{3,2,1,0:T(8,128)(2,1)}) fusion(bf16[4,1,640,768]{3,2,1,0:T(8,128)(2,1)} %param.8, f32[4,640]{1,0:T(4,128)S(1)} %mul.50, bf16[4,640,2048]{2,1,0:T(8,128)(2,1)} %bitcast.51, bf16[2048,4,768]{2,1,0:T(4,128)(2,1)} %param.9), kind=kOutput, calls=%fused_computation.10 | convolution fusion | flops 8062891520 | bytes 30953472 | tf_op jit(solution)/shard_map/esd,def->esf/dot_general | solution.py:112
  170.8 0.1 reshape.108
  170.9 0.7 copy.128
  171.6 5.1 %all-to-all-start = ((f32[4,32,20]{2,0,1:T(4,128)}), f32[4,32,20]{2,0,1:T(4,128)S(1)}, u32[]{:S(2)}, u32[]{:S(2)}) async-start(f32[4,32,20]{2,0,1:T(4,128)} %copy.128), calls=%async_computation.1 | async-start | bytes 131072 | tf_op jit(solution)/shard_map/all_to_all | solution.py:117
  176.7 7.3 %all-to-all-done = f32[4,32,20]{2,0,1:T(4,128)S(1)} async-done(((f32[4,32,20]{2,0,1:T(4,128)}), f32[4,32,20]{2,0,1:T(4,128)S(1)}, u32[]{:S(2)}, u32[]{:S(2)}) %all-to-all-start) | async-done | bytes 10272 | tf_op jit(solution)/shard_map/all_to_all | solution.py:117
  184.0 0.1 reshape.109
  184.1 6.2 %gather_fusion = f32[1024]{0:T(1024)S(1)} fusion(f32[2560]{0:T(1024)S(1)} %reshape.109, s32[1024]{0:T(1024)S(1)} %broadcast_clamp_fusion), kind=kCustom, calls=%fused_computation | custom fusion | bytes 12288 | tf_op jit(solution)/shard_map/jit(_take)/gather | solution.py:124
  190.4 0.7 copy.132
  191.1 71.9 %reduce-scatter.2.cloned.1.call-done = bf16[512,4,768]{0,2,1:T(8,128)(2,1)} async-done(((bf16[2048,4,768]{0,2,1:T(8,128)(2,1)}), bf16[512,4,768]{0,2,1:T(8,128)(2,1)}) %reduce-scatter.2.cloned.1.call-update) | async-done | bytes 3145744 | tf_op jit(solution)/shard_map/reduce_scatter | solution.py:104
  262.9 6.0 %copy.131 = bf16[512,4,768]{2,1,0:T(4,128)(2,1)} copy(bf16[512,4,768]{0,2,1:T(8,128)(2,1)} %reduce-scatter.2.cloned.1.call-done) | data formatting | bytes 6291456
  (27 shorter events, 0.7 us)
Async XLA Ops:
  7.2 82.4 %all-gather.3.cloned.1.call-start = ((), (), s32[]{:S(2)}) async-start(), calls=%async_computation.3 | async-start | bytes 18382848 | tf_op jit(solution)/shard_map/all_gather | solution.py:74
  10.7 252.2 %reduce-scatter.2.cloned.1.call-start = ((), (), s32[]{:S(2)}) async-start(), calls=%async_computation.2 | async-start | bytes 15728640 | tf_op jit(solution)/shard_map/reduce_scatter | solution.py:104
  149.2 0.7 copy-start
  171.6 12.4 %all-to-all-start = ((f32[4,32,20]{2,0,1:T(4,128)}), f32[4,32,20]{2,0,1:T(4,128)S(1)}, u32[]{:S(2)}, u32[]{:S(2)}) async-start(f32[4,32,20]{2,0,1:T(4,128)} %copy.128), calls=%async_computation.1 | async-start | bytes 131072 | tf_op jit(solution)/shard_map/all_to_all | solution.py:117
Sparse Core Ops, SparseCore 0:
  10.8 78.6 all-gather.2
  149.3 113.5 reduce-scatter.1

commit v3 on v2

--- a/solution.py
+++ b/solution.py
@@ -4,35 +4,39 @@
 from jax.experimental import pallas as pl
 from jax.sharding import PartitionSpec as P
 
+N_CHUNKS = 2
+
 
 def pick_kernel(column_ref, rows_ref, out_ref):
-    column = column_ref[0, 0]
-    group, tok, width = rows_ref.shape
+    column = column_ref[0]
+    group, tok, width = out_ref.shape[0], rows_ref.shape[1], out_ref.shape[3]
+    block = out_ref.shape[2]
     onehot = (
-        column == lax.broadcasted_iota(jnp.int32, (column.shape[0], group * tok), 1)
+        column == lax.broadcasted_iota(jnp.int32, (column.shape[0], rows_ref.shape[0] * tok), 1)
     ).astype(rows_ref.dtype)
-    rows = rows_ref[...].reshape(group * tok, width)
-    out_ref[0, 0] = jnp.dot(onehot, rows, preferred_element_type=jnp.float32).astype(
-        out_ref.dtype
-    )
+    rows = rows_ref[...].reshape(rows_ref.shape[0] * tok, width)
+    result = jnp.dot(onehot, rows, preferred_element_type=jnp.float32).astype(out_ref.dtype)
+    for j in range(group):
+        out_ref[j, 0] = result[j * block:(j + 1) * block]
 
 
-def pick(column, gathered, width):
-    local_experts, groups, block, _ = column.shape
+def pick(column, gathered, width, local):
+    groups, rows_per, _ = column.shape
     sources, tok, _ = gathered.shape
     group = sources // groups
+    block = rows_per // local
     return pl.pallas_call(
         pick_kernel,
-        out_shape=jax.ShapeDtypeStruct((local_experts, groups, block, width), gathered.dtype),
-        grid=(groups, local_experts),
+        out_shape=jax.ShapeDtypeStruct((local, groups, block, width), gathered.dtype),
+        grid=(groups,),
         in_specs=[
-            pl.BlockSpec((1, 1, block, 1), lambda g, j: (j, g, 0, 0)),
-            pl.BlockSpec((group, tok, width), lambda g, j: (g, 0, 0)),
+            pl.BlockSpec((1, rows_per, 1), lambda g: (g, 0, 0)),
+            pl.BlockSpec((group, tok, width), lambda g: (g, 0, 0)),
         ],
-        out_specs=pl.BlockSpec((1, 1, block, width), lambda g, j: (j, g, 0, 0)),
+        out_specs=pl.BlockSpec((local, 1, block, width), lambda g: (0, g, 0, 0)),
         cost_estimate=pl.CostEstimate(
-            flops=2 * local_experts * groups * block * group * tok * width,
-            bytes_accessed=sources * tok * width * 2 + local_experts * groups * block * width * 2,
+            flops=2 * groups * rows_per * group * tok * width,
+            bytes_accessed=sources * tok * width * 2 + groups * rows_per * width * 2,
             transcendentals=0,
         ),
     )(column, gathered)
@@ -61,19 +65,29 @@
     ) * capacity + position
     slot_index = slot_index.reshape(tok_rows, top_count)
 
+    piece = width // (replica_count * N_CHUNKS)
+    chunk_width = replica_count * piece
+    cols = grad_out.reshape(tok_rows, replica_count, N_CHUNKS, piece)
     extra = 128
-    info = jnp.concatenate(
+    first = jnp.concatenate(
         [
-            grad_out,
+            cols[:, :, 0, :].reshape(tok_rows, chunk_width),
             experts.astype(jnp.bfloat16),
             gates,
             jnp.zeros((tok_rows, extra - 2 * top_count), jnp.bfloat16),
         ],
         axis=1,
     )
-    gathered = lax.all_gather(info, "expert")
-    all_ids = gathered[:, :, width:width + top_count].astype(jnp.int32)
-    all_gates = gathered[:, :, width + top_count:width + 2 * top_count].astype(jnp.float32)
+    gathered = [lax.all_gather(first, "expert")]
+    for c in range(1, N_CHUNKS):
+        gathered.append(
+            lax.all_gather(cols[:, :, c, :].reshape(tok_rows, chunk_width), "expert")
+        )
+    head = gathered[0]
+    all_ids = head[:, :, chunk_width:chunk_width + top_count].astype(jnp.int32)
+    all_gates = head[:, :, chunk_width + top_count:chunk_width + 2 * top_count].astype(
+        jnp.float32
+    )
     pair_ids = all_ids.reshape(expert_count, tok_rows * top_count).T
     local_ids = pair_ids - me * local_experts
     mine = local_ids[:, :, None] == jnp.arange(local_experts, dtype=jnp.int32)[None, None, :]
@@ -93,25 +107,36 @@
     groups = expert_count // group
     within = (jnp.arange(expert_count, dtype=jnp.int32) % group * tok_rows)[:, None, None]
     column = jnp.where(owner >= 0, owner + within, -1)
-    column = jnp.transpose(column, (1, 0, 2)).reshape(
-        local_experts, groups, group * capacity, 1
-    )
-    grad_slots = pick(column, gathered, width).reshape(local_experts, slot_count, width)
+    column = jnp.transpose(column.reshape(groups, group, local_experts, capacity), (0, 2, 1, 3))
+    column = column.reshape(groups, local_experts * group * capacity, 1)
+    slot_parts = [
+        pick(column, part, chunk_width, local_experts).reshape(local_experts, slot_count, chunk_width)
+        for part in gathered
+    ]
 
     hidden_slots = hidden.reshape(local_experts, slot_count, hidden_width)
     weighted = (gate_slots[:, :, None] * hidden_slots.astype(jnp.float32)).astype(jnp.bfloat16)
 
-    down_grad = lax.psum_scatter(
-        jnp.einsum(
-            "esd,esf->def", grad_slots, weighted, preferred_element_type=jnp.float32
-        ).astype(jnp.bfloat16),
-        "replica",
-        scatter_dimension=0,
-        tiled=True,
-    )
-    upstream = jnp.einsum(
-        "esd,def->esf", grad_slots, down_weight, preferred_element_type=jnp.float32
-    )
+    rows = down_weight.reshape(replica_count, N_CHUNKS, piece, local_experts, hidden_width)
+    down_parts = []
+    upstream = None
+    for c, grad_slots in enumerate(slot_parts):
+        down_parts.append(
+            lax.psum_scatter(
+                jnp.einsum(
+                    "esd,esf->def", grad_slots, weighted, preferred_element_type=jnp.float32
+                ).astype(jnp.bfloat16),
+                "replica",
+                scatter_dimension=0,
+                tiled=True,
+            )
+        )
+        weight_rows = rows[:, c].reshape(chunk_width, local_experts, hidden_width)
+        part = jnp.einsum(
+            "esd,def->esf", grad_slots, weight_rows, preferred_element_type=jnp.float32
+        )
+        upstream = part if upstream is None else upstream + part
+    down_grad = jnp.concatenate(down_parts, axis=0)
     hidden_grad = (gate_slots[:, :, None] * upstream).astype(jnp.bfloat16).reshape(hidden.shape)
     slot_grad = jnp.sum(hidden_slots.astype(jnp.float32) * upstream, axis=2)
     returned = lax.all_to_all(

time: 278 us -> 296 us (1.065)
  local copies, waits for them, and re-layouts: 23.6 us -> 43.3 us
  Pallas kernels: 31 us -> 20.4 us
  matrix products: 36.3 us -> 40.9 us
  other arithmetic: 7.39 us -> 11.3 us
    all_gather x1 -> x2, waiting for transfers between devices: 78.7 us -> 96 us  [the longest x1 64.9 us: per_device(): gathered = [lax.all_gather(first, 'expert')]]
    reduce_scatter x1 -> x2, waiting for transfers between devices: 71.9 us -> 54.9 us  [per_device(): lax.psum_scatter(jnp.einsum('esd,esf->def', grad_slots, weighted, preferr...]
    all_gather x0 -> x1, local copies, waits for them, and re-layouts: none -> 12.5 us  [per_device(): gathered = [lax.all_gather(first, 'expert')]]
    pallas_call x1 -> x2, Pallas kernels: 31 us -> 20.4 us  [pick(): pl.pallas_call(pick_kernel, out_shape=jax.ShapeDtypeStruct((local, groups...]
    slice x0 -> x2, local copies, waits for them, and re-layouts: none -> 8.01 us  [the longest x1 7.98 us: per_device(): weight_rows = rows[:, c].reshape(chunk_width, local_experts, hidden_width)]
    concatenate x0 -> x2, other arithmetic: none -> 3.72 us  [the longest x1 2.1 us: per_device(): down_grad = jnp.concatenate(down_parts, axis=0)]
    dot_general x1 -> x2, matrix products: 16.8 us -> 20.5 us  [per_device(): jnp.einsum('esd,esf->def', grad_slots, weighted, preferred_element_type=j...]
    dot_general x1 -> x2, matrix products: 19.6 us -> 20.5 us  [per_device(): jnp.einsum('esd,def->esf', grad_slots, weight_rows, preferred_element_typ...]
  transfers between devices with their start and end apart: 3 -> 5, of which waited for: 3 -> 4; matrix products, arithmetic and copies ran while one was open for 10% -> 26% of each run, Pallas kernels for 0% -> 4%
where the time goes in v3:
time: 296 us; the launch traced here: 294 us
  waiting for transfers between devices  158 us (53%)
  local copies, waits for them, and re-layouts  43.3 us (15%)
  matrix products  40.9 us (14%)
  Pallas kernels  20.4 us (7%)
  between operations  14.1 us (5%)
  other arithmetic  11.3 us (4%)
  starting transfers between devices  6.05 us (2%)
    all_gather x1, waiting for transfers between devices, per_device(): gathered = [lax.all_gather(first, 'expert')]  64.9 us
    reduce_scatter x2, waiting for transfers between devices, per_device(): lax.psum_scatter(jnp.einsum('esd,esf->def', grad_slots, weighted, preferr...  54.9 us
    all_gather x1, waiting for transfers between devices, per_device(): lax.all_gather(cols[:, :, c, :].reshape(tok_rows, chunk_width), 'expert')  31 us
    dot_general x2, matrix products, per_device(): jnp.einsum('esd,def->esf', grad_slots, weight_rows, preferred_element_typ...  20.5 us
    dot_general x2, matrix products, per_device(): jnp.einsum('esd,esf->def', grad_slots, weighted, preferred_element_type=j...  20.5 us
    pallas_call x2, Pallas kernels, pick(): pl.pallas_call(pick_kernel, out_shape=jax.ShapeDtypeStruct((local, groups...  20.4 us
    all_gather x1, local copies, waits for them, and re-layouts, per_device(): gathered = [lax.all_gather(first, 'expert')]  12.5 us
    unnamed x8, local copies, waits for them, and re-layouts  8.39 us
  transfers between devices with their start and end apart: 5, of which 4 were waited for; matrix products, arithmetic and copies ran while one was open for 26% of the time, Pallas kernels for 4%

profile of v3, /device:TPU:1, one launch (start us, length us, event | category | flops | bytes accessed | tf_op | source)
XLA Modules:
  0.0 294.3 jit_solution(1222322171322853856)
XLA Ops:
  7.2 0.7 convert_element_type.40
  7.9 1.3 copy.150
  9.3 1.6 maximum_maximum_fusion
  11.0 0.9 copy.166
  12.1 64.9 %all-gather.6.cloned.1.call-done = bf16[4096,1152]{0,1:T(8,128)(2,1)} async-done(((bf16[128,1152]{0,1:T(8,128)(2,1)}), bf16[4096,1152]{0,1:T(8,128)(2,1)}) %all-gather.6.cloned.1.call-update) | async-done | bytes 9437200 | tf_op jit(solution)/shard_map/all_gather | solution.py:81
  77.0 12.5 %copy.151 = bf16[4096,1152]{1,0:T(8,128)(2,1)} copy(bf16[4096,1152]{0,1:T(8,128)(2,1)} %all-gather.6.cloned.1.call-done) | data formatting | bytes 18874368 | tf_op jit(solution)/shard_map/all_gather | solution.py:81
  89.6 1.6 convert_subtract_fusion
  91.1 1.0 copy.152
  92.2 0.2 copy.153
  92.4 0.1 eq.64
  92.5 0.2 eq.65
  92.7 0.1 convert_bitcast_fusion.2
  92.8 0.2 copy.154
  93.0 0.3 fusion.6
  93.6 0.2 copy.157
  93.8 0.1 eq.70
  94.0 0.3 copy.158
  94.3 1.4 select_reduce_fusion
  96.0 1.5 reshape.141.column_ref
  97.4 1.6 slice_convert_fusion
  99.1 1.0 copy.159
  100.1 0.2 copy.160
  100.3 1.1 select_reduce_fusion.1
  101.5 0.1 mul.50
  101.6 31.0 %all-gather.4.cloned.1.call-done.rows_ref = bf16[32,128,1024]{2,1,0:T(8,128)(2,1)} async-done(((bf16[1,128,1024]{2,1,0:T(8,128)(2,1)}), bf16[32,128,1024]{2,1,0:T(8,128)(2,1)}) %all-gather.4.cloned.1.call-update) | async-done | bytes 8388624 | tf_op jit(solution)/shard_map/all_gather | solution.py:84
  132.6 10.0 %shard_map.77 = bf16[4,8,80,1024]{3,2,1,0:T(8,128)(2,1)} custom-call(s32[8,320,1]{2,1,0:T(8,128)} %reshape.141.column_ref, bf16[32,128,1024]{2,1,0:T(8,128)(2,1)} %all-gather.4.cloned.1.call-done.rows_ref), custom_call_target="tpu_custom_call" | custom-call | flops 2684354560 | bytes 13631488 | tf_op jit(solution)/shard_map/pallas_call | solution.py:28
  142.6 10.2 %convert_bitcast_fusion = bf16[1024,4,768]{0,2,1:T(8,128)(2,1)} fusion(bf16[4,640,1024]{2,1,0:T(8,128)(2,1)} %bitcast.66, bf16[4,1,640,768]{3,2,1,0:T(8,128)(2,1)} %param.8, f32[4,640]{1,0:T(4,128)S(1)} %mul.50), kind=kOutput, calls=%fused_computation.9 | convolution fusion | flops 4035575808 | bytes 15476736 | tf_op jit(solution)/shard_map/esd,esf->def/dot_general | solution.py:126
  152.9 0.2 reduce-scatter.3.cloned.1.call-start
  153.1 10.4 %shard_map.76 = bf16[4,8,80,1024]{3,2,1,0:T(8,128)(2,1)} custom-call(s32[8,320,1]{2,1,0:T(8,128)} %reshape.141.column_ref, bf16[32,128,1152]{2,1,0:T(8,128)(2,1)} %bitcast.62), custom_call_target="tpu_custom_call" | custom-call | flops 2684354560 | bytes 13631488 | tf_op jit(solution)/shard_map/pallas_call | solution.py:28
  163.5 10.2 %convert_bitcast_fusion.1 = bf16[1024,4,768]{0,2,1:T(8,128)(2,1)} fusion(bf16[4,640,1024]{2,1,0:T(8,128)(2,1)} %bitcast.68, bf16[4,1,640,768]{3,2,1,0:T(8,128)(2,1)} %param.8, f32[4,640]{1,0:T(4,128)S(1)} %mul.50), kind=kOutput, calls=%fused_computation.10 | convolution fusion | flops 4035575808 | bytes 15476736 | tf_op jit(solution)/shard_map/esd,esf->def/dot_general | solution.py:126
  173.7 0.7 copy-done
  174.7 0.1 copy.178
  174.8 0.2 fusion.8
  175.2 0.2 copy.180
  175.7 8.0 %fusion.27 = (bf16[4,1,256,4,768]{4,3,2,1,0:T(4,128)(2,1)S(1)}, bf16[4,1,256,4,768]{4,3,2,1,0:T(4,128)(2,1)S(1)}) fusion(bf16[4,2,256,4,768]{4,3,2,1,0:T(4,128)(2,1)} %bitcast.63), kind=kLoop, calls=%fused_computation.67 | loop fusion | bytes 25165824 | tf_op jit(solution)/shard_map/slice | solution.py:134
  183.7 1.0 copy.189
  184.8 1.0 copy.188
  185.8 8.7 %fusion.29 = f32[4,640,768]{2,1,0:T(8,128)} fusion(bf16[4,640,1024]{2,1,0:T(8,128)(2,1)} %bitcast.69, bf16[1024,4,768]{2,0,1:T(8,128)(2,1)S(1)} %bitcast.65), kind=kOutput, calls=%fused_computation.69 | convolution fusion | flops 4026531840 | bytes 19398656 | tf_op jit(solution)/shard_map/esd,def->esf/dot_general | solution.py:135
  194.5 11.7 %fusion.1 = (f32[4,640]{1,0:T(4,128)S(1)}, bf16[4,1,640,768]{3,2,1,0:T(8,128)(2,1)}) fusion(bf16[4,1,640,768]{3,2,1,0:T(8,128)(2,1)} %param.8, f32[4,640,768]{2,1,0:T(8,128)} %fusion.29, f32[4,640]{1,0:T(4,128)S(1)} %mul.50, bf16[4,640,1024]{2,1,0:T(8,128)(2,1)} %bitcast.67, bf16[1024,4,768]{2,0,1:T(8,128)(2,1)S(1)} %bitcast.64), kind=kOutput, calls=%fused_computation.7 | convolution fusion | flops 4038325760 | bytes 27283456 | tf_op jit(solution)/shard_map/esd,def->esf/dot_general | solution.py:135
  206.3 0.1 reshape.126
  206.4 0.7 copy.181
  207.1 5.7 %all-to-all-start = ((f32[4,32,20]{2,0,1:T(4,128)}), f32[4,32,20]{2,0,1:T(4,128)S(1)}, u32[]{:S(2)}, u32[]{:S(2)}) async-start(f32[4,32,20]{2,0,1:T(4,128)} %copy.181), calls=%async_computation.2 | async-start | bytes 131072 | tf_op jit(solution)/shard_map/all_to_all | solution.py:142
  212.8 7.3 %all-to-all-done = f32[4,32,20]{2,0,1:T(4,128)S(1)} async-done(((f32[4,32,20]{2,0,1:T(4,128)}), f32[4,32,20]{2,0,1:T(4,128)S(1)}, u32[]{:S(2)}, u32[]{:S(2)}) %all-to-all-start) | async-done | bytes 10272 | tf_op jit(solution)/shard_map/all_to_all | solution.py:142
  220.2 6.2 %gather_fusion = f32[1024]{0:T(1024)S(1)} fusion(f32[2560]{0:T(1024)S(1)} %reshape.127, s32[1024]{0:T(1024)S(1)} %broadcast_clamp_fusion), kind=kCustom, calls=%fused_computation | custom fusion | bytes 12288 | tf_op jit(solution)/shard_map/jit(_take)/gather | solution.py:149
  226.5 0.7 copy.185
  227.1 54.9 %reduce-scatter.3.cloned.1.call-done = bf16[256,4,768]{0,2,1:T(8,128)(2,1)} async-done(((bf16[1024,4,768]{0,2,1:T(8,128)(2,1)}), bf16[256,4,768]{0,2,1:T(8,128)(2,1)}) %reduce-scatter.3.cloned.1.call-update) | async-done | bytes 1572880 | tf_op jit(solution)/shard_map/reduce_scatter | solution.py:125
  282.1 2.1 pad_maximum_fusion
  284.2 3.6 %copy.184 = bf16[512,4,768]{2,1,0:T(4,128)(2,1)} copy(bf16[512,4,768]{0,2,1:T(8,128)(2,1)S(1)} %pad_maximum_fusion) | data formatting | bytes 6291456
  (45 shorter events, 2.0 us)
Async XLA Ops:
  7.2 69.9 %all-gather.6.cloned.1.call-start = ((), (), s32[]{:S(2)}) async-start(), calls=%async_computation.6 | async-start | bytes 9732096 | tf_op jit(solution)/shard_map/all_gather | solution.py:81
  11.0 121.6 %all-gather.4.cloned.1.call-start = ((), (), s32[]{:S(2)}) async-start(), calls=%async_computation.3 | async-start | bytes 8650752 | tf_op jit(solution)/shard_map/all_gather | solution.py:84
  11.9 215.2 %reduce-scatter.5.cloned.1.call-start = ((), (), s32[]{:S(2)}) async-start(), calls=%async_computation.5 | async-start | bytes 7864320 | tf_op jit(solution)/shard_map/reduce_scatter | solution.py:125
  152.9 129.2 %reduce-scatter.3.cloned.1.call-start = ((), (), s32[]{:S(2)}) async-start(), calls=%async_computation.4 | async-start | bytes 7864320 | tf_op jit(solution)/shard_map/reduce_scatter | solution.py:125
  173.7 0.7 copy-start
  207.1 13.0 %all-to-all-start = ((f32[4,32,20]{2,0,1:T(4,128)}), f32[4,32,20]{2,0,1:T(4,128)S(1)}, u32[]{:S(2)}, u32[]{:S(2)}) async-start(f32[4,32,20]{2,0,1:T(4,128)} %copy.181), calls=%async_computation.2 | async-start | bytes 131072 | tf_op jit(solution)/shard_map/all_to_all | solution.py:142
Sparse Core Ops, SparseCore 0:
  11.1 65.8 all-gather.5
  79.9 52.6 all-gather.3
  153.0 63.1 reduce-scatter.4
  218.4 63.6 reduce-scatter.2

commit v4 on v2

--- a/solution.py
+++ b/solution.py
@@ -6,33 +6,35 @@
 
 
 def pick_kernel(column_ref, rows_ref, out_ref):
-    column = column_ref[0, 0]
-    group, tok, width = rows_ref.shape
+    column = column_ref[0]
+    local, _, block, width = out_ref.shape
+    group, tok, _ = rows_ref.shape
     onehot = (
         column == lax.broadcasted_iota(jnp.int32, (column.shape[0], group * tok), 1)
     ).astype(rows_ref.dtype)
     rows = rows_ref[...].reshape(group * tok, width)
-    out_ref[0, 0] = jnp.dot(onehot, rows, preferred_element_type=jnp.float32).astype(
-        out_ref.dtype
-    )
+    result = jnp.dot(onehot, rows, preferred_element_type=jnp.float32).astype(out_ref.dtype)
+    for j in range(local):
+        out_ref[j, 0] = result[j * block:(j + 1) * block]
 
 
-def pick(column, gathered, width):
-    local_experts, groups, block, _ = column.shape
+def pick(column, gathered, width, local):
+    groups, rows_per, _ = column.shape
     sources, tok, _ = gathered.shape
     group = sources // groups
+    block = rows_per // local
     return pl.pallas_call(
         pick_kernel,
-        out_shape=jax.ShapeDtypeStruct((local_experts, groups, block, width), gathered.dtype),
-        grid=(groups, local_experts),
+        out_shape=jax.ShapeDtypeStruct((local, groups, block, width), gathered.dtype),
+        grid=(groups,),
         in_specs=[
-            pl.BlockSpec((1, 1, block, 1), lambda g, j: (j, g, 0, 0)),
-            pl.BlockSpec((group, tok, width), lambda g, j: (g, 0, 0)),
+            pl.BlockSpec((1, rows_per, 1), lambda g: (g, 0, 0)),
+            pl.BlockSpec((group, tok, width), lambda g: (g, 0, 0)),
         ],
-        out_specs=pl.BlockSpec((1, 1, block, width), lambda g, j: (j, g, 0, 0)),
+        out_specs=pl.BlockSpec((local, 1, block, width), lambda g: (0, g, 0, 0)),
         cost_estimate=pl.CostEstimate(
-            flops=2 * local_experts * groups * block * group * tok * width,
-            bytes_accessed=sources * tok * width * 2 + local_experts * groups * block * width * 2,
+            flops=2 * groups * rows_per * group * tok * width,
+            bytes_accessed=sources * tok * width * 2 + groups * rows_per * width * 2,
             transcendentals=0,
         ),
     )(column, gathered)
@@ -93,10 +95,11 @@
     groups = expert_count // group
     within = (jnp.arange(expert_count, dtype=jnp.int32) % group * tok_rows)[:, None, None]
     column = jnp.where(owner >= 0, owner + within, -1)
-    column = jnp.transpose(column, (1, 0, 2)).reshape(
-        local_experts, groups, group * capacity, 1
+    column = jnp.transpose(column.reshape(groups, group, local_experts, capacity), (0, 2, 1, 3))
+    column = column.reshape(groups, local_experts * group * capacity, 1)
+    grad_slots = pick(column, gathered, width, local_experts).reshape(
+        local_experts, slot_count, width
     )
-    grad_slots = pick(column, gathered, width).reshape(local_experts, slot_count, width)
 
     hidden_slots = hidden.reshape(local_experts, slot_count, hidden_width)
     weighted = (gate_slots[:, :, None] * hidden_slots.astype(jnp.float32)).astype(jnp.bfloat16)

time: 278 us -> 260 us (0.935)
  Pallas kernels: 31 us -> 15.1 us
    pallas_call x1, Pallas kernels: 31 us -> 15.1 us  [pick(): pl.pallas_call(pick_kernel, out_shape=jax.ShapeDtypeStruct((local, groups...]
  transfers between devices with their start and end apart: 3 -> 3, of which waited for: 3 -> 3; matrix products, arithmetic and copies ran while one was open for 10% -> 11% of each run, Pallas kernels for 0% -> 0%
where the time goes in v4:
time: 260 us
  waiting for transfers between devices  158 us (61%)
  matrix products  36.3 us (14%)
  local copies, waits for them, and re-layouts  23.7 us (9%)
  Pallas kernels  15.1 us (6%)
  between operations  14.3 us (6%)
  other arithmetic  7.48 us (3%)
  starting transfers between devices  5.15 us (2%)
    all_gather x1, waiting for transfers between devices, per_device(): gathered = lax.all_gather(info, 'expert')  78.6 us
    reduce_scatter x1, waiting for transfers between devices, per_device(): lax.psum_scatter(jnp.einsum('esd,esf->def', grad_slots, weighted, preferr...  71.8 us
    dot_general x1, matrix products, per_device(): jnp.einsum('esd,def->esf', grad_slots, down_weight, preferred_element_typ...  19.6 us
    dot_general x1, matrix products, per_device(): jnp.einsum('esd,esf->def', grad_slots, weighted, preferred_element_type=j...  16.8 us
    pallas_call x1, Pallas kernels, pick(): pl.pallas_call(pick_kernel, out_shape=jax.ShapeDtypeStruct((local, groups...  15.1 us
    unnamed x6, local copies, waits for them, and re-layouts  8.18 us
    all_to_all x1, waiting for transfers between devices, per_device(): lax.all_to_all(slot_grad.reshape(local_experts, expert_count, capacity),...  7.31 us
    gather x2, local copies, waits for them, and re-layouts, per_device(): gate_grad = jnp.take(returned.reshape(-1), slot_index, axis=0)  6.23 us
  transfers between devices with their start and end apart: 3, of which 3 were waited for; matrix products, arithmetic and copies ran while one was open for 11% of the time, Pallas kernels for 0%

profile of v4, /device:TPU:1, one launch (start us, length us, event | category | flops | bytes accessed | tf_op | source)
XLA Modules:
  0.0 259.9 jit_solution(15127511925590447222)
XLA Ops:
  7.2 0.7 convert_element_type.34
  7.9 0.1 copy.105
  8.0 0.8 copy.106
  8.8 1.9 concatenate.3
  10.8 0.1 eq.67
  10.9 78.6 %all-gather.3.cloned.1.call-done = bf16[4096,2176]{1,0:T(8,128)(2,1)} async-done(((bf16[128,2176]{1,0:T(8,128)(2,1)}), bf16[4096,2176]{1,0:T(8,128)(2,1)}) %all-gather.3.cloned.1.call-update) | async-done | bytes 17825808 | tf_op jit(solution)/shard_map/all_gather | solution.py:76
  89.6 1.6 slice_convert_fusion
  91.2 1.0 copy.114
  92.2 0.2 copy.115
  92.4 1.5 convert_subtract_fusion
  93.9 1.0 copy.107
  94.9 0.2 copy.108
  95.1 0.1 eq.64
  95.3 0.2 eq.65
  95.5 0.1 convert_bitcast_fusion.1
  95.6 0.2 copy.109
  95.8 0.3 fusion.9
  96.2 0.1 copy.111
  96.3 0.2 copy.112
  96.6 0.1 eq.70
  96.7 0.3 copy.113
  97.1 1.1 select_reduce_fusion.1
  98.2 0.1 copy.116
  98.3 0.1 mul.50
  98.4 1.5 select_reduce_fusion
  99.8 0.1 copy.117
  100.0 1.5 reshape.129.column_ref
  101.5 15.1 %shard_map.76 = bf16[4,8,80,2048]{3,2,1,0:T(8,128)(2,1)} custom-call(s32[8,320,1]{2,1,0:T(8,128)} %reshape.129.column_ref, bf16[32,128,2176]{2,1,0:T(8,128)(2,1)} %bitcast.50), custom_call_target="tpu_custom_call" | custom-call | flops 5368709120 | bytes 27262976 | tf_op jit(solution)/shard_map/pallas_call | solution.py:26
  116.6 16.8 %convert_bitcast_fusion = bf16[2048,4,768]{0,2,1:T(8,128)(2,1)} fusion(bf16[4,640,2048]{2,1,0:T(8,128)(2,1)} %bitcast.51, bf16[4,1,640,768]{3,2,1,0:T(8,128)(2,1)} %param.8, f32[4,640]{1,0:T(4,128)S(1)} %mul.50), kind=kOutput, calls=%fused_computation.3 | convolution fusion | flops 8065253376 | bytes 27011072 | tf_op jit(solution)/shard_map/esd,esf->def/dot_general | solution.py:108
  133.4 0.7 copy-done
  134.1 0.1 copy.123
  134.2 0.1 eq.78
  134.3 0.1 eq.74
  134.4 0.1 copy.129
  134.5 0.2 fusion.11
  134.8 0.1 copy.130
  134.9 0.2 copy.131
  135.3 0.1 reshape.120
  135.4 19.6 %fusion.3 = (f32[4,640]{1,0:T(4,128)S(1)}, bf16[4,1,640,768]{3,2,1,0:T(8,128)(2,1)}) fusion(bf16[4,1,640,768]{3,2,1,0:T(8,128)(2,1)} %param.8, f32[4,640]{1,0:T(4,128)S(1)} %mul.50, bf16[4,640,2048]{2,1,0:T(8,128)(2,1)} %bitcast.52, bf16[2048,4,768]{2,1,0:T(4,128)(2,1)} %param.9), kind=kOutput, calls=%fused_computation.10 | convolution fusion | flops 8062891520 | bytes 30953472 | tf_op jit(solution)/shard_map/esd,def->esf/dot_general | solution.py:115
  155.0 0.1 reshape.114
  155.1 0.7 copy.132
  155.8 5.1 %all-to-all-start = ((f32[4,32,20]{2,0,1:T(4,128)}), f32[4,32,20]{2,0,1:T(4,128)S(1)}, u32[]{:S(2)}, u32[]{:S(2)}) async-start(f32[4,32,20]{2,0,1:T(4,128)} %copy.132), calls=%async_computation.1 | async-start | bytes 131072 | tf_op jit(solution)/shard_map/all_to_all | solution.py:120
  160.9 7.3 %all-to-all-done = f32[4,32,20]{2,0,1:T(4,128)S(1)} async-done(((f32[4,32,20]{2,0,1:T(4,128)}), f32[4,32,20]{2,0,1:T(4,128)S(1)}, u32[]{:S(2)}, u32[]{:S(2)}) %all-to-all-start) | async-done | bytes 10272 | tf_op jit(solution)/shard_map/all_to_all | solution.py:120
  168.2 0.1 reshape.115
  168.3 6.2 %gather_fusion = f32[1024]{0:T(1024)S(1)} fusion(f32[2560]{0:T(1024)S(1)} %reshape.115, s32[1024]{0:T(1024)S(1)} %broadcast_clamp_fusion), kind=kCustom, calls=%fused_computation | custom fusion | bytes 12288 | tf_op jit(solution)/shard_map/jit(_take)/gather | solution.py:127
  174.6 0.7 copy.136
  175.2 71.8 %reduce-scatter.2.cloned.1.call-done = bf16[512,4,768]{0,2,1:T(8,128)(2,1)} async-done(((bf16[2048,4,768]{0,2,1:T(8,128)(2,1)}), bf16[512,4,768]{0,2,1:T(8,128)(2,1)}) %reduce-scatter.2.cloned.1.call-update) | async-done | bytes 3145744 | tf_op jit(solution)/shard_map/reduce_scatter | solution.py:107
  247.1 6.0 %copy.135 = bf16[512,4,768]{2,1,0:T(4,128)(2,1)} copy(bf16[512,4,768]{0,2,1:T(8,128)(2,1)} %reduce-scatter.2.cloned.1.call-done) | data formatting | bytes 6291456
  (29 shorter events, 0.8 us)
Async XLA Ops:
  7.2 82.4 %all-gather.3.cloned.1.call-start = ((), (), s32[]{:S(2)}) async-start(), calls=%async_computation.3 | async-start | bytes 18382848 | tf_op jit(solution)/shard_map/all_gather | solution.py:76
  10.7 236.4 %reduce-scatter.2.cloned.1.call-start = ((), (), s32[]{:S(2)}) async-start(), calls=%async_computation.2 | async-start | bytes 15728640 | tf_op jit(solution)/shard_map/reduce_scatter | solution.py:107
  133.4 0.7 copy-start
  155.8 12.4 %all-to-all-start = ((f32[4,32,20]{2,0,1:T(4,128)}), f32[4,32,20]{2,0,1:T(4,128)S(1)}, u32[]{:S(2)}, u32[]{:S(2)}) async-start(f32[4,32,20]{2,0,1:T(4,128)} %copy.132), calls=%async_computation.1 | async-start | bytes 131072 | tf_op jit(solution)/shard_map/all_to_all | solution.py:120
Sparse Core Ops, SparseCore 0:
  10.8 78.6 all-gather.2
  133.5 113.4 reduce-scatter.1

commit v5 on v4

--- a/solution.py
+++ b/solution.py
@@ -63,19 +63,13 @@
     ) * capacity + position
     slot_index = slot_index.reshape(tok_rows, top_count)
 
-    extra = 128
-    info = jnp.concatenate(
-        [
-            grad_out,
-            experts.astype(jnp.bfloat16),
-            gates,
-            jnp.zeros((tok_rows, extra - 2 * top_count), jnp.bfloat16),
-        ],
-        axis=1,
-    )
-    gathered = lax.all_gather(info, "expert")
-    all_ids = gathered[:, :, width:width + top_count].astype(jnp.int32)
-    all_gates = gathered[:, :, width + top_count:width + 2 * top_count].astype(jnp.float32)
+    info = jnp.concatenate([experts.astype(jnp.float32), gates.astype(jnp.float32)], axis=1)
+    info = jnp.broadcast_to(info.reshape(1, -1), (expert_count, tok_rows * 2 * top_count))
+    info = lax.all_to_all(info, "expert", split_axis=0, concat_axis=0, tiled=True)
+    info = info.reshape(expert_count, tok_rows, 2 * top_count)
+    all_ids = info[:, :, :top_count].astype(jnp.int32)
+    all_gates = info[:, :, top_count:]
+    gathered = lax.all_gather(grad_out, "expert")
     pair_ids = all_ids.reshape(expert_count, tok_rows * top_count).T
     local_ids = pair_ids - me * local_experts
     mine = local_ids[:, :, None] == jnp.arange(local_experts, dtype=jnp.int32)[None, None, :]

time: 260 us -> 245 us (0.942)
  waiting for transfers between devices: 158 us -> 139 us
  starting transfers between devices: 5.15 us -> 14.6 us
  local copies, waits for them, and re-layouts: 23.7 us -> 20.2 us
    all_gather x1, waiting for transfers between devices: 78.6 us -> 50.7 us  [per_device(): gathered = lax.all_gather(grad_out, 'expert')]
    all_to_all x0 -> x1, starting transfers between devices: none -> 9.43 us  [per_device(): lax.all_to_all(info, 'expert', split_axis=0, concat_axis=0, tiled=True)]
    all_to_all x0 -> x1, waiting for transfers between devices: none -> 8.71 us  [per_device(): lax.all_to_all(info, 'expert', split_axis=0, concat_axis=0, tiled=True)]
    unnamed x6 -> x5, local copies, waits for them, and re-layouts: 8.18 us -> 7.38 us
  transfers between devices with their start and end apart: 3 -> 4, of which waited for: 3 -> 4; matrix products, arithmetic and copies ran while one was open for 11% -> 16% of each run, Pallas kernels for 0% -> 0%
where the time goes in v5:
time: 245 us
  waiting for transfers between devices  139 us (57%)
  matrix products  36.3 us (15%)
  local copies, waits for them, and re-layouts  20.2 us (8%)
  Pallas kernels  15.1 us (6%)
  starting transfers between devices  14.6 us (6%)
  between operations  14.3 us (6%)
  other arithmetic  5.12 us (2%)
    reduce_scatter x1, waiting for transfers between devices, per_device(): lax.psum_scatter(jnp.einsum('esd,esf->def', grad_slots, weighted, preferr...  71.8 us
    all_gather x1, waiting for transfers between devices, per_device(): gathered = lax.all_gather(grad_out, 'expert')  50.7 us
    dot_general x1, matrix products, per_device(): jnp.einsum('esd,def->esf', grad_slots, down_weight, preferred_element_typ...  19.5 us
    dot_general x1, matrix products, per_device(): jnp.einsum('esd,esf->def', grad_slots, weighted, preferred_element_type=j...  16.8 us
    pallas_call x1, Pallas kernels, pick(): pl.pallas_call(pick_kernel, out_shape=jax.ShapeDtypeStruct((local, groups...  15.1 us
    all_to_all x1, starting transfers between devices, per_device(): lax.all_to_all(info, 'expert', split_axis=0, concat_axis=0, tiled=True)  9.43 us
    all_to_all x1, waiting for transfers between devices, per_device(): lax.all_to_all(info, 'expert', split_axis=0, concat_axis=0, tiled=True)  8.71 us
    unnamed x5, local copies, waits for them, and re-layouts  7.38 us
  transfers between devices with their start and end apart: 4, of which 4 were waited for; matrix products, arithmetic and copies ran while one was open for 16% of the time, Pallas kernels for 0%

profile of v5, /device:TPU:1, one launch (start us, length us, event | category | flops | bytes accessed | tf_op | source)
XLA Modules:
  0.0 245.0 jit_solution(16452667534151110929)
XLA Ops:
  7.2 0.7 all-gather.3.cloned.1.call-update
  7.9 0.7 convert_element_type.36
  8.6 0.7 convert_element_type.37
  9.3 0.1 copy.66
  9.5 0.8 broadcast_in_dim.51
  10.3 9.4 %all-to-all-start = ((f32[32,1,2048]{2,1,0:T(1,128)}), f32[32,1,2048]{2,1,0:T(1,128)S(1)}, u32[]{:S(2)}, u32[]{:S(2)}) async-start(f32[32,1,2048]{2,1,0:T(1,128)} %broadcast_in_dim.51), calls=%async_computation | async-start | bytes 524288 | tf_op jit(solution)/shard_map/all_to_all | solution.py:68
  19.8 0.1 eq.67
  19.9 8.7 %all-to-all-done = f32[32,1,2048]{2,1,0:T(1,128)S(1)} async-done(((f32[32,1,2048]{2,1,0:T(1,128)}), f32[32,1,2048]{2,1,0:T(1,128)S(1)}, u32[]{:S(2)}, u32[]{:S(2)}) %all-to-all-start) | async-done | bytes 262176 | tf_op jit(solution)/shard_map/all_to_all | solution.py:68
  28.7 0.3 copy.67
  29.1 0.2 copy.68
  29.2 0.1 eq.64
  29.4 0.2 eq.65
  29.6 0.1 convert_bitcast_fusion.1
  29.7 0.2 copy.69
  29.9 0.3 fusion.11
  30.3 0.1 copy.71
  30.4 0.2 copy.72
  30.7 0.1 eq.70
  30.9 0.3 copy.73
  31.2 0.2 copy.74
  31.4 1.1 select_reduce_fusion.1
  32.5 0.1 copy.75
  32.6 0.1 mul.50
  32.7 1.5 select_reduce_fusion
  34.2 0.1 copy.76
  34.4 1.5 reshape.141.column_ref
  35.9 50.7 %all-gather.3.cloned.1.call-done = bf16[4096,2048]{1,0:T(8,128)(2,1)} async-done(((bf16[128,2048]{1,0:T(8,128)(2,1)}), bf16[4096,2048]{1,0:T(8,128)(2,1)}) %all-gather.3.cloned.1.call-update) | async-done | bytes 16777232 | tf_op jit(solution)/shard_map/all_gather | solution.py:72
  86.5 15.1 %shard_map.76 = bf16[4,8,80,2048]{3,2,1,0:T(8,128)(2,1)} custom-call(s32[8,320,1]{2,1,0:T(8,128)} %reshape.141.column_ref, bf16[32,128,2048]{2,1,0:T(8,128)(2,1)} %bitcast.51), custom_call_target="tpu_custom_call" | custom-call | flops 5368709120 | bytes 27262976 | tf_op jit(solution)/shard_map/pallas_call | solution.py:26
  101.7 16.8 %convert_bitcast_fusion = bf16[2048,4,768]{0,2,1:T(8,128)(2,1)} fusion(bf16[4,640,2048]{2,1,0:T(8,128)(2,1)} %bitcast.52, bf16[4,1,640,768]{3,2,1,0:T(8,128)(2,1)} %param.8, f32[4,640]{1,0:T(4,128)S(1)} %mul.50), kind=kOutput, calls=%fused_computation.3 | convolution fusion | flops 8065253376 | bytes 27011072 | tf_op jit(solution)/shard_map/esd,esf->def/dot_general | solution.py:102
  118.5 0.7 copy-done
  119.1 0.1 copy.82
  119.2 0.1 eq.78
  119.3 0.1 eq.74
  119.4 0.1 copy.88
  119.5 0.2 fusion.13
  119.8 0.1 copy.89
  119.9 0.2 copy.90
  120.4 0.1 reshape.132
  120.5 19.5 %fusion.3 = (f32[4,640]{1,0:T(4,128)S(1)}, bf16[4,1,640,768]{3,2,1,0:T(8,128)(2,1)}) fusion(bf16[4,1,640,768]{3,2,1,0:T(8,128)(2,1)} %param.8, f32[4,640]{1,0:T(4,128)S(1)} %mul.50, bf16[4,640,2048]{2,1,0:T(8,128)(2,1)} %bitcast.53, bf16[2048,4,768]{2,1,0:T(4,128)(2,1)} %param.9), kind=kOutput, calls=%fused_computation.10 | convolution fusion | flops 8062891520 | bytes 30953472 | tf_op jit(solution)/shard_map/esd,def->esf/dot_general | solution.py:109
  140.0 0.1 reshape.127
  140.2 0.7 copy.91
  140.8 5.1 %all-to-all-start.1 = ((f32[4,32,20]{2,0,1:T(4,128)}), f32[4,32,20]{2,0,1:T(4,128)S(1)}, u32[]{:S(2)}, u32[]{:S(2)}) async-start(f32[4,32,20]{2,0,1:T(4,128)} %copy.91), calls=%async_computation.2 | async-start | bytes 131072 | tf_op jit(solution)/shard_map/all_to_all | solution.py:114
  146.0 7.3 %all-to-all-done.1 = f32[4,32,20]{2,0,1:T(4,128)S(1)} async-done(((f32[4,32,20]{2,0,1:T(4,128)}), f32[4,32,20]{2,0,1:T(4,128)S(1)}, u32[]{:S(2)}, u32[]{:S(2)}) %all-to-all-start.1) | async-done | bytes 10272 | tf_op jit(solution)/shard_map/all_to_all | solution.py:114
  153.3 0.1 reshape.128
  153.4 6.2 %gather_fusion = f32[1024]{0:T(1024)S(1)} fusion(f32[2560]{0:T(1024)S(1)} %reshape.128, s32[1024]{0:T(1024)S(1)} %broadcast_clamp_fusion), kind=kCustom, calls=%fused_computation | custom fusion | bytes 12288 | tf_op jit(solution)/shard_map/jit(_take)/gather | solution.py:121
  159.7 0.7 copy.95
  160.3 71.8 %reduce-scatter.2.cloned.1.call-done = bf16[512,4,768]{0,2,1:T(8,128)(2,1)} async-done(((bf16[2048,4,768]{0,2,1:T(8,128)(2,1)}), bf16[512,4,768]{0,2,1:T(8,128)(2,1)}) %reduce-scatter.2.cloned.1.call-update) | async-done | bytes 3145744 | tf_op jit(solution)/shard_map/reduce_scatter | solution.py:101
  232.2 6.0 %copy.94 = bf16[512,4,768]{2,1,0:T(4,128)(2,1)} copy(bf16[512,4,768]{0,2,1:T(8,128)(2,1)} %reduce-scatter.2.cloned.1.call-done) | data formatting | bytes 6291456
  (31 shorter events, 0.9 us)
Async XLA Ops:
  7.2 79.4 %all-gather.3.cloned.1.call-start = ((), (), s32[]{:S(2)}) async-start(), calls=%async_computation.4 | async-start | bytes 17301504 | tf_op jit(solution)/shard_map/all_gather | solution.py:72
  10.3 18.4 %all-to-all-start = ((f32[32,1,2048]{2,1,0:T(1,128)}), f32[32,1,2048]{2,1,0:T(1,128)S(1)}, u32[]{:S(2)}, u32[]{:S(2)}) async-start(f32[32,1,2048]{2,1,0:T(1,128)} %broadcast_in_dim.51), calls=%async_computation | async-start | bytes 524288 | tf_op jit(solution)/shard_map/all_to_all | solution.py:68
  19.7 212.4 %reduce-scatter.2.cloned.1.call-start = ((), (), s32[]{:S(2)}) async-start(), calls=%async_computation.3 | async-start | bytes 15728640 | tf_op jit(solution)/shard_map/reduce_scatter | solution.py:101
  118.5 0.7 copy-start
  140.8 12.5 %all-to-all-start.1 = ((f32[4,32,20]{2,0,1:T(4,128)}), f32[4,32,20]{2,0,1:T(4,128)S(1)}, u32[]{:S(2)}, u32[]{:S(2)}) async-start(f32[4,32,20]{2,0,1:T(4,128)} %copy.91), calls=%async_computation.2 | async-start | bytes 131072 | tf_op jit(solution)/shard_map/all_to_all | solution.py:114
Sparse Core Ops, SparseCore 0:
  10.3 76.2 all-gather.2
  118.6 113.5 reduce-scatter.1

commit v6 on v5

--- a/solution.py
+++ b/solution.py
@@ -100,12 +100,13 @@
 
     down_grad = lax.psum_scatter(
         jnp.einsum(
-            "esd,esf->def", grad_slots, weighted, preferred_element_type=jnp.float32
+            "esd,esf->edf", grad_slots, weighted, preferred_element_type=jnp.float32
         ).astype(jnp.bfloat16),
         "replica",
-        scatter_dimension=0,
+        scatter_dimension=1,
         tiled=True,
     )
+    down_grad = jnp.transpose(down_grad, (1, 0, 2))
     upstream = jnp.einsum(
         "esd,def->esf", grad_slots, down_weight, preferred_element_type=jnp.float32
     )

time: 245 us -> 246 us (level)
  no operation moved by 1% of the time
where the time goes in v6:
time: 246 us; the launch traced here: 245 us
  waiting for transfers between devices  139 us (57%)
  matrix products  36.9 us (15%)
  local copies, waits for them, and re-layouts  20.2 us (8%)
  Pallas kernels  15.1 us (6%)
  starting transfers between devices  14.4 us (6%)
  between operations  14.3 us (6%)
  other arithmetic  5.12 us (2%)
    reduce_scatter x1, waiting for transfers between devices, per_device(): lax.psum_scatter(jnp.einsum('esd,esf->edf', grad_slots, weighted, preferr...  71.6 us
    all_gather x1, waiting for transfers between devices, per_device(): gathered = lax.all_gather(grad_out, 'expert')  50.7 us
    dot_general x1, matrix products, per_device(): jnp.einsum('esd,def->esf', grad_slots, down_weight, preferred_element_typ...  20 us
    dot_general x1, matrix products, per_device(): jnp.einsum('esd,esf->edf', grad_slots, weighted, preferred_element_type=j...  16.9 us
    pallas_call x1, Pallas kernels, pick(): pl.pallas_call(pick_kernel, out_shape=jax.ShapeDtypeStruct((local, groups...  15.1 us
    all_to_all x1, starting transfers between devices, per_device(): lax.all_to_all(info, 'expert', split_axis=0, concat_axis=0, tiled=True)  9.43 us
    all_to_all x1, waiting for transfers between devices, per_device(): lax.all_to_all(info, 'expert', split_axis=0, concat_axis=0, tiled=True)  8.71 us
    unnamed x5, local copies, waits for them, and re-layouts  7.4 us
  transfers between devices with their start and end apart: 4, of which 4 were waited for; matrix products, arithmetic and copies ran while one was open for 16% of the time, Pallas kernels for 0%

profile of v6, /device:TPU:1, one launch (start us, length us, event | category | flops | bytes accessed | tf_op | source)
XLA Modules:
  0.0 245.1 jit_solution(7269681309972034445)
XLA Ops:
  7.2 0.7 all-gather.3.cloned.1.call-update
  7.9 0.7 convert_element_type.33
  8.6 0.7 convert_element_type.34
  9.3 0.1 copy.66
  9.5 0.8 broadcast_in_dim.51
  10.3 9.4 %all-to-all-start = ((f32[32,1,2048]{2,1,0:T(1,128)}), f32[32,1,2048]{2,1,0:T(1,128)S(1)}, u32[]{:S(2)}, u32[]{:S(2)}) async-start(f32[32,1,2048]{2,1,0:T(1,128)} %broadcast_in_dim.51), calls=%async_computation | async-start | bytes 524288 | tf_op jit(solution)/shard_map/all_to_all | solution.py:68
  19.8 0.1 eq.67
  19.9 8.7 %all-to-all-done = f32[32,1,2048]{2,1,0:T(1,128)S(1)} async-done(((f32[32,1,2048]{2,1,0:T(1,128)}), f32[32,1,2048]{2,1,0:T(1,128)S(1)}, u32[]{:S(2)}, u32[]{:S(2)}) %all-to-all-start) | async-done | bytes 262176 | tf_op jit(solution)/shard_map/all_to_all | solution.py:68
  28.7 0.3 copy.67
  29.1 0.2 copy.68
  29.2 0.1 eq.64
  29.4 0.2 eq.65
  29.6 0.1 convert_bitcast_fusion
  29.7 0.2 copy.69
  29.9 0.3 fusion.11
  30.3 0.1 copy.71
  30.4 0.2 copy.72
  30.7 0.1 eq.70
  30.9 0.3 copy.73
  31.2 0.2 copy.74
  31.4 1.1 select_reduce_fusion.1
  32.5 0.1 copy.75
  32.6 0.1 mul.50
  32.7 1.5 select_reduce_fusion
  34.2 0.1 copy.76
  34.4 1.5 reshape.141.column_ref
  35.9 50.7 %all-gather.3.cloned.1.call-done = bf16[4096,2048]{1,0:T(8,128)(2,1)} async-done(((bf16[128,2048]{1,0:T(8,128)(2,1)}), bf16[4096,2048]{1,0:T(8,128)(2,1)}) %all-gather.3.cloned.1.call-update) | async-done | bytes 16777232 | tf_op jit(solution)/shard_map/all_gather | solution.py:72
  86.5 15.1 %shard_map.76 = bf16[4,8,80,2048]{3,2,1,0:T(8,128)(2,1)} custom-call(s32[8,320,1]{2,1,0:T(8,128)} %reshape.141.column_ref, bf16[32,128,2048]{2,1,0:T(8,128)(2,1)} %bitcast.50), custom_call_target="tpu_custom_call" | custom-call | flops 5368709120 | bytes 27262976 | tf_op jit(solution)/shard_map/pallas_call | solution.py:26
  101.7 16.9 %convolution_convert_fusion = bf16[4,2048,768]{2,1,0:T(8,128)(2,1)} fusion(bf16[4,640,2048]{2,1,0:T(8,128)(2,1)} %bitcast.51, bf16[4,1,640,768]{3,2,1,0:T(8,128)(2,1)} %param.8, f32[4,640]{1,0:T(4,128)S(1)} %mul.50), kind=kOutput, calls=%fused_computation.11 | convolution fusion | flops 8065253376 | bytes 27011072 | tf_op jit(solution)/shard_map/esd,esf->edf/dot_general | solution.py:102
  118.6 0.7 copy-done
  119.3 0.1 copy.82
  119.4 0.1 eq.78
  119.5 0.1 eq.74
  119.5 0.1 copy.88
  119.6 0.2 fusion.13
  119.9 0.1 copy.89
  120.1 0.2 copy.90
  120.5 0.1 reshape.132
  120.6 20.0 %fusion.3 = (f32[4,640]{1,0:T(4,128)S(1)}, bf16[4,1,640,768]{3,2,1,0:T(8,128)(2,1)}) fusion(bf16[4,1,640,768]{3,2,1,0:T(8,128)(2,1)} %param.8, f32[4,640]{1,0:T(4,128)S(1)} %mul.50, bf16[4,640,2048]{2,1,0:T(8,128)(2,1)} %bitcast.52, bf16[2048,4,768]{2,1,0:T(4,128)(2,1)} %param.9), kind=kOutput, calls=%fused_computation.9 | convolution fusion | flops 8062891520 | bytes 30953472 | tf_op jit(solution)/shard_map/esd,def->esf/dot_general | solution.py:110
  140.6 0.1 reshape.127
  140.7 0.7 copy.91
  141.4 4.9 %all-to-all-start.1 = ((f32[4,32,20]{2,0,1:T(4,128)}), f32[4,32,20]{2,0,1:T(4,128)S(1)}, u32[]{:S(2)}, u32[]{:S(2)}) async-start(f32[4,32,20]{2,0,1:T(4,128)} %copy.91), calls=%async_computation.2 | async-start | bytes 131072 | tf_op jit(solution)/shard_map/all_to_all | solution.py:115
  146.3 7.3 %all-to-all-done.1 = f32[4,32,20]{2,0,1:T(4,128)S(1)} async-done(((f32[4,32,20]{2,0,1:T(4,128)}), f32[4,32,20]{2,0,1:T(4,128)S(1)}, u32[]{:S(2)}, u32[]{:S(2)}) %all-to-all-start.1) | async-done | bytes 10272 | tf_op jit(solution)/shard_map/all_to_all | solution.py:115
  153.6 0.1 reshape.128
  153.7 6.2 %gather_fusion = f32[1024]{0:T(1024)S(1)} fusion(f32[2560]{0:T(1024)S(1)} %reshape.128, s32[1024]{0:T(1024)S(1)} %broadcast_clamp_fusion), kind=kCustom, calls=%fused_computation | custom fusion | bytes 12288 | tf_op jit(solution)/shard_map/jit(_take)/gather | solution.py:122
  160.0 0.7 copy.95
  160.7 71.6 %reduce-scatter.2.cloned.1.call-done = bf16[4,512,768]{2,1,0:T(8,128)(2,1)} async-done(((bf16[4,2048,768]{2,1,0:T(8,128)(2,1)}), bf16[4,512,768]{2,1,0:T(8,128)(2,1)}) %reduce-scatter.2.cloned.1.call-update) | async-done | bytes 3145744 | tf_op jit(solution)/shard_map/reduce_scatter | solution.py:101
  232.3 6.0 %copy.94 = bf16[512,4,768]{2,1,0:T(4,128)(2,1)} copy(bf16[512,4,768]{2,0,1:T(8,128)(2,1)} %bitcast.55) | data formatting | bytes 6291456
  (31 shorter events, 0.9 us)
Async XLA Ops:
  7.2 79.4 %all-gather.3.cloned.1.call-start = ((), (), s32[]{:S(2)}) async-start(), calls=%async_computation.4 | async-start | bytes 17301504 | tf_op jit(solution)/shard_map/all_gather | solution.py:72
  10.3 18.4 %all-to-all-start = ((f32[32,1,2048]{2,1,0:T(1,128)}), f32[32,1,2048]{2,1,0:T(1,128)S(1)}, u32[]{:S(2)}, u32[]{:S(2)}) async-start(f32[32,1,2048]{2,1,0:T(1,128)} %broadcast_in_dim.51), calls=%async_computation | async-start | bytes 524288 | tf_op jit(solution)/shard_map/all_to_all | solution.py:68
  19.7 212.5 %reduce-scatter.2.cloned.1.call-start = ((), (), s32[]{:S(2)}) async-start(), calls=%async_computation.3 | async-start | bytes 15728640 | tf_op jit(solution)/shard_map/reduce_scatter | solution.py:101
  118.6 0.7 copy-start
  141.4 12.2 %all-to-all-start.1 = ((f32[4,32,20]{2,0,1:T(4,128)}), f32[4,32,20]{2,0,1:T(4,128)S(1)}, u32[]{:S(2)}, u32[]{:S(2)}) async-start(f32[4,32,20]{2,0,1:T(4,128)} %copy.91), calls=%async_computation.2 | async-start | bytes 131072 | tf_op jit(solution)/shard_map/all_to_all | solution.py:115
Sparse Core Ops, SparseCore 0:
  10.3 76.2 all-gather.2
  118.7 113.5 reduce-scatter.1

commit v7 on v6

--- a/solution.py
+++ b/solution.py
@@ -85,7 +85,7 @@
     gate_slots = jnp.sum(jnp.where(hit, gate_pairs[:, :, None, None], 0.0), axis=0)
     gate_slots = jnp.transpose(gate_slots, (1, 0, 2)).reshape(local_experts, slot_count)
 
-    group = 4
+    group = 2
     groups = expert_count // group
     within = (jnp.arange(expert_count, dtype=jnp.int32) % group * tok_rows)[:, None, None]
     column = jnp.where(owner >= 0, owner + within, -1)

time: 246 us -> 249 us (1.012)
  Pallas kernels: 15.1 us -> 17.8 us
    pallas_call x1, Pallas kernels: 15.1 us -> 17.8 us  [pick(): pl.pallas_call(pick_kernel, out_shape=jax.ShapeDtypeStruct((local, groups...]
where the time goes in v7:
time: 249 us; the launch traced here: 248 us
  waiting for transfers between devices  139 us (56%)
  matrix products  36.4 us (15%)
  local copies, waits for them, and re-layouts  20.4 us (8%)
  Pallas kernels  17.8 us (7%)
  starting transfers between devices  14.7 us (6%)
  between operations  14.3 us (6%)
  other arithmetic  5.12 us (2%)
    reduce_scatter x1, waiting for transfers between devices, per_device(): lax.psum_scatter(jnp.einsum('esd,esf->edf', grad_slots, weighted, preferr...  71.8 us
    all_gather x1, waiting for transfers between devices, per_device(): gathered = lax.all_gather(grad_out, 'expert')  50.4 us
    dot_general x1, matrix products, per_device(): jnp.einsum('esd,def->esf', grad_slots, down_weight, preferred_element_typ...  19.5 us
    pallas_call x1, Pallas kernels, pick(): pl.pallas_call(pick_kernel, out_shape=jax.ShapeDtypeStruct((local, groups...  17.8 us
    dot_general x1, matrix products, per_device(): jnp.einsum('esd,esf->edf', grad_slots, weighted, preferred_element_type=j...  16.9 us
    all_to_all x1, starting transfers between devices, per_device(): lax.all_to_all(info, 'expert', split_axis=0, concat_axis=0, tiled=True)  9.43 us
    all_to_all x1, waiting for transfers between devices, per_device(): lax.all_to_all(info, 'expert', split_axis=0, concat_axis=0, tiled=True)  8.71 us
    unnamed x5, local copies, waits for them, and re-layouts  7.4 us
  transfers between devices with their start and end apart: 4, of which 4 were waited for; matrix products, arithmetic and copies ran while one was open for 16% of the time, Pallas kernels for 0%

profile of v7, /device:TPU:1, one launch (start us, length us, event | category | flops | bytes accessed | tf_op | source)
XLA Modules:
  0.0 247.8 jit_solution(6787972220676522752)
XLA Ops:
  7.2 0.7 all-gather.3.cloned.1.call-update
  7.9 0.7 convert_element_type.33
  8.6 0.7 convert_element_type.34
  9.3 0.1 copy.66
  9.5 0.8 broadcast_in_dim.51
  10.3 9.4 %all-to-all-start = ((f32[32,1,2048]{2,1,0:T(1,128)}), f32[32,1,2048]{2,1,0:T(1,128)S(1)}, u32[]{:S(2)}, u32[]{:S(2)}) async-start(f32[32,1,2048]{2,1,0:T(1,128)} %broadcast_in_dim.51), calls=%async_computation | async-start | bytes 524288 | tf_op jit(solution)/shard_map/all_to_all | solution.py:68
  19.8 0.1 eq.67
  19.9 8.7 %all-to-all-done = f32[32,1,2048]{2,1,0:T(1,128)S(1)} async-done(((f32[32,1,2048]{2,1,0:T(1,128)}), f32[32,1,2048]{2,1,0:T(1,128)S(1)}, u32[]{:S(2)}, u32[]{:S(2)}) %all-to-all-start) | async-done | bytes 262176 | tf_op jit(solution)/shard_map/all_to_all | solution.py:68
  28.7 0.3 copy.67
  29.1 0.2 copy.68
  29.2 0.1 eq.64
  29.4 0.2 eq.65
  29.6 0.1 convert_bitcast_fusion
  29.7 0.2 copy.69
  29.9 0.3 fusion.11
  30.3 0.1 copy.71
  30.4 0.2 copy.72
  30.7 0.1 eq.70
  30.9 0.3 copy.73
  31.2 0.2 copy.74
  31.4 1.1 select_reduce_fusion.1
  32.5 0.1 copy.75
  32.6 0.1 mul.50
  32.7 1.5 select_reduce_fusion
  34.2 0.1 copy.76
  34.3 0.1 fusion.20
  34.4 1.7 reshape.141.column_ref
  36.1 50.4 %all-gather.3.cloned.1.call-done = bf16[4096,2048]{1,0:T(8,128)(2,1)} async-done(((bf16[128,2048]{1,0:T(8,128)(2,1)}), bf16[4096,2048]{1,0:T(8,128)(2,1)}) %all-gather.3.cloned.1.call-update) | async-done | bytes 16777232 | tf_op jit(solution)/shard_map/all_gather | solution.py:72
  86.5 17.8 %shard_map.76 = bf16[4,16,40,2048]{3,2,1,0:T(8,128)(2,1)} custom-call(s32[16,160,1]{2,1,0:T(8,128)} %reshape.141.column_ref, bf16[32,128,2048]{2,1,0:T(8,128)(2,1)} %bitcast.50), custom_call_target="tpu_custom_call" | custom-call | flops 2684354560 | bytes 27262976 | tf_op jit(solution)/shard_map/pallas_call | solution.py:26
  104.3 16.9 %convolution_convert_fusion = bf16[4,2048,768]{2,1,0:T(8,128)(2,1)} fusion(bf16[4,640,2048]{2,1,0:T(8,128)(2,1)} %bitcast.51, bf16[4,1,640,768]{3,2,1,0:T(8,128)(2,1)} %param.8, f32[4,640]{1,0:T(4,128)S(1)} %mul.50), kind=kOutput, calls=%fused_computation.11 | convolution fusion | flops 8065253376 | bytes 27011072 | tf_op jit(solution)/shard_map/esd,esf->edf/dot_general | solution.py:102
  121.2 0.7 copy-done
  121.9 0.1 copy.82
  122.0 0.1 eq.78
  122.2 0.1 copy.88
  122.3 0.2 fusion.13
  122.6 0.1 copy.89
  122.7 0.2 copy.90
  123.1 0.1 reshape.132
  123.2 19.5 %fusion.3 = (f32[4,640]{1,0:T(4,128)S(1)}, bf16[4,1,640,768]{3,2,1,0:T(8,128)(2,1)}) fusion(bf16[4,1,640,768]{3,2,1,0:T(8,128)(2,1)} %param.8, f32[4,640]{1,0:T(4,128)S(1)} %mul.50, bf16[4,640,2048]{2,1,0:T(8,128)(2,1)} %bitcast.52, bf16[2048,4,768]{2,1,0:T(4,128)(2,1)} %param.9), kind=kOutput, calls=%fused_computation.9 | convolution fusion | flops 8062891520 | bytes 30953472 | tf_op jit(solution)/shard_map/esd,def->esf/dot_general | solution.py:110
  142.8 0.1 reshape.127
  142.9 0.7 copy.91
  143.5 5.2 %all-to-all-start.1 = ((f32[4,32,20]{2,0,1:T(4,128)}), f32[4,32,20]{2,0,1:T(4,128)S(1)}, u32[]{:S(2)}, u32[]{:S(2)}) async-start(f32[4,32,20]{2,0,1:T(4,128)} %copy.91), calls=%async_computation.2 | async-start | bytes 131072 | tf_op jit(solution)/shard_map/all_to_all | solution.py:115
  148.7 7.3 %all-to-all-done.1 = f32[4,32,20]{2,0,1:T(4,128)S(1)} async-done(((f32[4,32,20]{2,0,1:T(4,128)}), f32[4,32,20]{2,0,1:T(4,128)S(1)}, u32[]{:S(2)}, u32[]{:S(2)}) %all-to-all-start.1) | async-done | bytes 10272 | tf_op jit(solution)/shard_map/all_to_all | solution.py:115
  156.1 0.1 reshape.128
  156.2 6.2 %gather_fusion = f32[1024]{0:T(1024)S(1)} fusion(f32[2560]{0:T(1024)S(1)} %reshape.128, s32[1024]{0:T(1024)S(1)} %broadcast_clamp_fusion), kind=kCustom, calls=%fused_computation | custom fusion | bytes 12288 | tf_op jit(solution)/shard_map/jit(_take)/gather | solution.py:122
  162.4 0.7 copy.95
  163.1 71.8 %reduce-scatter.2.cloned.1.call-done = bf16[4,512,768]{2,1,0:T(8,128)(2,1)} async-done(((bf16[4,2048,768]{2,1,0:T(8,128)(2,1)}), bf16[4,512,768]{2,1,0:T(8,128)(2,1)}) %reduce-scatter.2.cloned.1.call-update) | async-done | bytes 3145744 | tf_op jit(solution)/shard_map/reduce_scatter | solution.py:101
  234.9 6.0 %copy.94 = bf16[512,4,768]{2,1,0:T(4,128)(2,1)} copy(bf16[512,4,768]{2,0,1:T(8,128)(2,1)} %bitcast.55) | data formatting | bytes 6291456
  (31 shorter events, 1.0 us)
Async XLA Ops:
  7.2 79.4 %all-gather.3.cloned.1.call-start = ((), (), s32[]{:S(2)}) async-start(), calls=%async_computation.4 | async-start | bytes 17301504 | tf_op jit(solution)/shard_map/all_gather | solution.py:72
  10.3 18.4 %all-to-all-start = ((f32[32,1,2048]{2,1,0:T(1,128)}), f32[32,1,2048]{2,1,0:T(1,128)S(1)}, u32[]{:S(2)}, u32[]{:S(2)}) async-start(f32[32,1,2048]{2,1,0:T(1,128)} %broadcast_in_dim.51), calls=%async_computation | async-start | bytes 524288 | tf_op jit(solution)/shard_map/all_to_all | solution.py:68
  19.7 215.2 %reduce-scatter.2.cloned.1.call-start = ((), (), s32[]{:S(2)}) async-start(), calls=%async_computation.3 | async-start | bytes 15728640 | tf_op jit(solution)/shard_map/reduce_scatter | solution.py:101
  121.2 0.7 copy-start
  143.5 12.5 %all-to-all-start.1 = ((f32[4,32,20]{2,0,1:T(4,128)}), f32[4,32,20]{2,0,1:T(4,128)S(1)}, u32[]{:S(2)}, u32[]{:S(2)}) async-start(f32[4,32,20]{2,0,1:T(4,128)} %copy.91), calls=%async_computation.2 | async-start | bytes 131072 | tf_op jit(solution)/shard_map/all_to_all | solution.py:115
Sparse Core Ops, SparseCore 0:
  10.3 76.2 all-gather.2
  121.3 113.5 reduce-scatter.1

commit v8 on v5

--- a/solution.py
+++ b/solution.py
@@ -5,39 +5,42 @@
 from jax.sharding import PartitionSpec as P
 
 
-def pick_kernel(column_ref, rows_ref, out_ref):
+def pick_kernel(column_ref, mine_ref, theirs_ref, out_ref):
     column = column_ref[0]
     local, _, block, width = out_ref.shape
-    group, tok, _ = rows_ref.shape
+    pair, tok, _ = mine_ref.shape
+    half = pair * tok
     onehot = (
-        column == lax.broadcasted_iota(jnp.int32, (column.shape[0], group * tok), 1)
-    ).astype(rows_ref.dtype)
-    rows = rows_ref[...].reshape(group * tok, width)
-    result = jnp.dot(onehot, rows, preferred_element_type=jnp.float32).astype(out_ref.dtype)
+        column == lax.broadcasted_iota(jnp.int32, (column.shape[0], 2 * half), 1)
+    ).astype(mine_ref.dtype)
+    result = jnp.dot(
+        onehot[:, :half], mine_ref[...].reshape(half, width), preferred_element_type=jnp.float32
+    ) + jnp.dot(
+        onehot[:, half:], theirs_ref[...].reshape(half, width), preferred_element_type=jnp.float32
+    )
+    result = result.astype(out_ref.dtype)
     for j in range(local):
         out_ref[j, 0] = result[j * block:(j + 1) * block]
 
 
-def pick(column, gathered, width, local):
+def pick(column, mine, theirs, local):
     groups, rows_per, _ = column.shape
-    sources, tok, _ = gathered.shape
-    group = sources // groups
+    chips, tok, width = mine.shape
+    pair = chips // groups
     block = rows_per // local
+    spec = pl.BlockSpec((pair, tok, width), lambda g: (g, 0, 0))
     return pl.pallas_call(
         pick_kernel,
-        out_shape=jax.ShapeDtypeStruct((local, groups, block, width), gathered.dtype),
+        out_shape=jax.ShapeDtypeStruct((local, groups, block, width), mine.dtype),
         grid=(groups,),
-        in_specs=[
-            pl.BlockSpec((1, rows_per, 1), lambda g: (g, 0, 0)),
-            pl.BlockSpec((group, tok, width), lambda g: (g, 0, 0)),
-        ],
+        in_specs=[pl.BlockSpec((1, rows_per, 1), lambda g: (g, 0, 0)), spec, spec],
         out_specs=pl.BlockSpec((local, 1, block, width), lambda g: (0, g, 0, 0)),
         cost_estimate=pl.CostEstimate(
-            flops=2 * groups * rows_per * group * tok * width,
-            bytes_accessed=sources * tok * width * 2 + groups * rows_per * width * 2,
+            flops=4 * groups * rows_per * pair * tok * width,
+            bytes_accessed=2 * chips * tok * width * 2 + groups * rows_per * width * 2,
             transcendentals=0,
         ),
-    )(column, gathered)
+    )(column, mine, theirs)
 
 
 def per_device(grad_out, gates, experts, hidden, down_weight):
@@ -69,7 +72,12 @@
     info = info.reshape(expert_count, tok_rows, 2 * top_count)
     all_ids = info[:, :, :top_count].astype(jnp.int32)
     all_gates = info[:, :, top_count:]
-    gathered = lax.all_gather(grad_out, "expert")
+    cores = 2
+    core_groups = [list(range(c, expert_count, cores)) for c in range(cores)]
+    mine_rows = lax.all_gather(grad_out, "expert", axis_index_groups=core_groups)
+    theirs_rows = lax.ppermute(
+        mine_rows, "expert", [(i, i ^ 1) for i in range(expert_count)]
+    )
     pair_ids = all_ids.reshape(expert_count, tok_rows * top_count).T
     local_ids = pair_ids - me * local_experts
     mine = local_ids[:, :, None] == jnp.arange(local_experts, dtype=jnp.int32)[None, None, :]
@@ -87,11 +95,13 @@
 
     group = 4
     groups = expert_count // group
-    within = (jnp.arange(expert_count, dtype=jnp.int32) % group * tok_rows)[:, None, None]
+    source = jnp.arange(expert_count, dtype=jnp.int32)
+    other = (source % cores != me % cores).astype(jnp.int32)
+    within = ((other * (group // cores) + source % group // cores) * tok_rows)[:, None, None]
     column = jnp.where(owner >= 0, owner + within, -1)
     column = jnp.transpose(column.reshape(groups, group, local_experts, capacity), (0, 2, 1, 3))
     column = column.reshape(groups, local_experts * group * capacity, 1)
-    grad_slots = pick(column, gathered, width, local_experts).reshape(
+    grad_slots = pick(column, mine_rows, theirs_rows, local_experts).reshape(
         local_experts, slot_count, width
     )
 

time: 245 us -> 266 us (1.086)
  waiting for transfers between devices: 139 us -> 164 us
  starting transfers between devices: 14.6 us -> 9.91 us
    all_gather x1, waiting for transfers between devices: 50.7 us -> 76.3 us  [per_device(): lax.all_gather(grad_out, 'expert', axis_index_groups=core_groups)]
    all_to_all x1, starting transfers between devices: 9.43 us -> 5.42 us  [per_device(): lax.all_to_all(info, 'expert', split_axis=0, concat_axis=0, tiled=True)]
  transfers between devices with their start and end apart: 4 -> 5, of which waited for: 4 -> 4; matrix products, arithmetic and copies ran while one was open for 16% -> 15% of each run, Pallas kernels for 0% -> 0%
where the time goes in v8:
time: 266 us; the launch traced here: 265 us
  waiting for transfers between devices  164 us (62%)
  matrix products  37.2 us (14%)
  local copies, waits for them, and re-layouts  20.2 us (8%)
  Pallas kernels  14.8 us (6%)
  between operations  14.4 us (5%)
  starting transfers between devices  9.91 us (4%)
  other arithmetic  5.12 us (2%)
    all_gather x1, waiting for transfers between devices, per_device(): lax.all_gather(grad_out, 'expert', axis_index_groups=core_groups)  76.3 us
    reduce_scatter x1, waiting for transfers between devices, per_device(): lax.psum_scatter(jnp.einsum('esd,esf->def', grad_slots, weighted, preferr...  70.6 us
    dot_general x1, matrix products, per_device(): jnp.einsum('esd,def->esf', grad_slots, down_weight, preferred_element_typ...  20.4 us
    dot_general x1, matrix products, per_device(): jnp.einsum('esd,esf->def', grad_slots, weighted, preferred_element_type=j...  16.8 us
    pallas_call x1, Pallas kernels, pick(): pl.pallas_call(pick_kernel, out_shape=jax.ShapeDtypeStruct((local, groups...  14.8 us
    all_to_all x1, waiting for transfers between devices, per_device(): lax.all_to_all(info, 'expert', split_axis=0, concat_axis=0, tiled=True)  8.68 us
    all_to_all x1, waiting for transfers between devices, per_device(): lax.all_to_all(slot_grad.reshape(local_experts, expert_count, capacity),...  7.42 us
    unnamed x5, local copies, waits for them, and re-layouts  7.38 us
  transfers between devices with their start and end apart: 5, of which 4 were waited for; matrix products, arithmetic and copies ran while one was open for 15% of the time, Pallas kernels for 0%

profile of v8, /device:TPU:1, one launch (start us, length us, event | category | flops | bytes accessed | tf_op | source)
XLA Modules:
  0.0 265.3 jit_solution(9887811073798245848)
XLA Ops:
  7.2 0.7 all-gather.3.cloned.1.call-update
  7.9 76.3 %all-gather.3.cloned.1.call-done = bf16[2048,2048]{1,0:T(8,128)(2,1)} async-done(((bf16[128,2048]{1,0:T(8,128)(2,1)}), bf16[2048,2048]{1,0:T(8,128)(2,1)}) %all-gather.3.cloned.1.call-update) | async-done | bytes 8388624 | tf_op jit(solution)/shard_map/all_gather | solution.py:77
  84.2 0.7 collective-permute-start
  84.9 0.7 convert_element_type.38
  85.6 0.7 convert_element_type.37
  86.3 0.1 copy.66
  86.5 0.8 broadcast_in_dim.51
  87.3 5.4 %all-to-all-start = ((f32[32,1,2048]{2,1,0:T(1,128)}), f32[32,1,2048]{2,1,0:T(1,128)S(1)}, u32[]{:S(2)}, u32[]{:S(2)}) async-start(f32[32,1,2048]{2,1,0:T(1,128)} %broadcast_in_dim.51), calls=%async_computation | async-start | bytes 524288 | tf_op jit(solution)/shard_map/all_to_all | solution.py:71
  92.8 0.1 eq.70
  93.0 8.7 %all-to-all-done = f32[32,1,2048]{2,1,0:T(1,128)S(1)} async-done(((f32[32,1,2048]{2,1,0:T(1,128)}), f32[32,1,2048]{2,1,0:T(1,128)S(1)}, u32[]{:S(2)}, u32[]{:S(2)}) %all-to-all-start) | async-done | bytes 262176 | tf_op jit(solution)/shard_map/all_to_all | solution.py:71
  101.7 0.3 copy.67
  102.1 0.2 copy.74
  102.3 0.2 copy.68
  102.5 0.1 eq.67
  102.6 0.2 eq.68
  102.8 0.1 convert_bitcast_fusion.1
  103.0 0.2 copy.69
  103.1 0.3 fusion.11
  103.6 0.1 copy.71
  103.7 0.2 copy.72
  103.9 0.1 eq.73
  104.1 0.3 copy.73
  104.4 1.1 select_reduce_fusion.1
  105.5 0.1 copy.75
  105.6 0.1 mul.54
  105.7 1.5 select_reduce_fusion
  107.2 0.1 copy.76
  107.4 1.5 reshape.167.column_ref
  108.9 14.8 %shard_map.76 = bf16[4,8,80,2048]{3,2,1,0:T(8,128)(2,1)} custom-call(s32[8,320,1]{2,1,0:T(8,128)} %reshape.167.column_ref, bf16[16,128,2048]{2,1,0:T(8,128)(2,1)} %bitcast.54, bf16[16,128,2048]{2,1,0:T(8,128)(2,1)} %collective-permute-done.theirs_ref), custom_call_target="tpu_custom_call" | custom-call | flops 5368709120 | bytes 27262976 | tf_op jit(solution)/shard_map/pallas_call | solution.py:32
  123.7 16.8 %convert_bitcast_fusion = bf16[2048,4,768]{0,2,1:T(8,128)(2,1)} fusion(bf16[4,640,2048]{2,1,0:T(8,128)(2,1)} %bitcast.51, bf16[4,1,640,768]{3,2,1,0:T(8,128)(2,1)} %param.8, f32[4,640]{1,0:T(4,128)S(1)} %mul.54), kind=kOutput, calls=%fused_computation.3 | convolution fusion | flops 8065253376 | bytes 27011072 | tf_op jit(solution)/shard_map/esd,esf->def/dot_general | solution.py:112
  140.5 0.7 copy-done
  141.1 0.1 copy.82
  141.2 0.1 eq.81
  141.3 0.1 eq.77
  141.4 0.1 copy.88
  141.5 0.2 fusion.13
  141.8 0.1 copy.89
  141.9 0.2 copy.90
  142.5 20.4 %fusion.3 = (f32[4,640]{1,0:T(4,128)S(1)}, bf16[4,1,640,768]{3,2,1,0:T(8,128)(2,1)}) fusion(bf16[4,1,640,768]{3,2,1,0:T(8,128)(2,1)} %param.8, f32[4,640]{1,0:T(4,128)S(1)} %mul.54, bf16[4,640,2048]{2,1,0:T(8,128)(2,1)} %bitcast.52, bf16[2048,4,768]{2,1,0:T(4,128)(2,1)} %param.9), kind=kOutput, calls=%fused_computation.10 | convolution fusion | flops 8062891520 | bytes 30953472 | tf_op jit(solution)/shard_map/esd,def->esf/dot_general | solution.py:119
  162.9 0.1 reshape.153
  163.0 0.7 copy.91
  163.7 3.7 %all-to-all-start.1 = ((f32[4,32,20]{2,0,1:T(4,128)}), f32[4,32,20]{2,0,1:T(4,128)S(1)}, u32[]{:S(2)}, u32[]{:S(2)}) async-start(f32[4,32,20]{2,0,1:T(4,128)} %copy.91), calls=%async_computation.2 | async-start | bytes 131072 | tf_op jit(solution)/shard_map/all_to_all | solution.py:124
  167.4 7.4 %all-to-all-done.1 = f32[4,32,20]{2,0,1:T(4,128)S(1)} async-done(((f32[4,32,20]{2,0,1:T(4,128)}), f32[4,32,20]{2,0,1:T(4,128)S(1)}, u32[]{:S(2)}, u32[]{:S(2)}) %all-to-all-start.1) | async-done | bytes 10272 | tf_op jit(solution)/shard_map/all_to_all | solution.py:124
  174.9 0.1 reshape.154
  175.0 6.2 %gather_fusion = f32[1024]{0:T(1024)S(1)} fusion(f32[2560]{0:T(1024)S(1)} %reshape.154, s32[1024]{0:T(1024)S(1)} %broadcast_clamp_fusion), kind=kCustom, calls=%fused_computation | custom fusion | bytes 12288 | tf_op jit(solution)/shard_map/jit(_take)/gather | solution.py:131
  181.3 0.7 copy.95
  181.9 70.6 %reduce-scatter.2.cloned.1.call-done = bf16[512,4,768]{0,2,1:T(8,128)(2,1)} async-done(((bf16[2048,4,768]{0,2,1:T(8,128)(2,1)}), bf16[512,4,768]{0,2,1:T(8,128)(2,1)}) %reduce-scatter.2.cloned.1.call-update) | async-done | bytes 3145744 | tf_op jit(solution)/shard_map/reduce_scatter | solution.py:111
  252.6 6.0 %copy.94 = bf16[512,4,768]{2,1,0:T(4,128)(2,1)} copy(bf16[512,4,768]{0,2,1:T(8,128)(2,1)} %reduce-scatter.2.cloned.1.call-done) | data formatting | bytes 6291456
  (33 shorter events, 1.0 us)
Async XLA Ops:
  7.2 77.1 %all-gather.3.cloned.1.call-start = ((), (), s32[]{:S(2)}) async-start(), calls=%async_computation.4 | async-start | bytes 8912896 | tf_op jit(solution)/shard_map/all_gather | solution.py:77
  84.2 24.6 %collective-permute-start = (bf16[16,128,2048]{2,1,0:T(8,128)(2,1)}, bf16[16,128,2048]{2,1,0:T(8,128)(2,1)}, u32[]{:S(2)}, u32[]{:S(2)}) collective-permute-start(bf16[16,128,2048]{2,1,0:T(8,128)(2,1)} %bitcast.53), channel_id=1, source_target_pairs={{0,4},{4,0},{8,12},{12,8},{16,20},{20,16},{24,28},{28,24},{32,36},... | collective-permute-start | bytes 25165832 | tf_op jit(solution)/shard_map/ppermute | solution.py:78
  87.3 14.3 %all-to-all-start = ((f32[32,1,2048]{2,1,0:T(1,128)}), f32[32,1,2048]{2,1,0:T(1,128)S(1)}, u32[]{:S(2)}, u32[]{:S(2)}) async-start(f32[32,1,2048]{2,1,0:T(1,128)} %broadcast_in_dim.51), calls=%async_computation | async-start | bytes 524288 | tf_op jit(solution)/shard_map/all_to_all | solution.py:71
  92.8 159.8 %reduce-scatter.2.cloned.1.call-start = ((), (), s32[]{:S(2)}) async-start(), calls=%async_computation.3 | async-start | bytes 15728640 | tf_op jit(solution)/shard_map/reduce_scatter | solution.py:111
  140.5 0.7 copy-start
  163.7 11.2 %all-to-all-start.1 = ((f32[4,32,20]{2,0,1:T(4,128)}), f32[4,32,20]{2,0,1:T(4,128)S(1)}, u32[]{:S(2)}, u32[]{:S(2)}) async-start(f32[4,32,20]{2,0,1:T(4,128)} %copy.91), calls=%async_computation.2 | async-start | bytes 131072 | tf_op jit(solution)/shard_map/all_to_all | solution.py:124
Sparse Core Ops, SparseCore 0:
  10.1 74.0 all-gather.2
  140.6 111.8 reduce-scatter.1

commit v9 on v5

--- a/solution.py
+++ b/solution.py
@@ -85,7 +85,7 @@
     gate_slots = jnp.sum(jnp.where(hit, gate_pairs[:, :, None, None], 0.0), axis=0)
     gate_slots = jnp.transpose(gate_slots, (1, 0, 2)).reshape(local_experts, slot_count)
 
-    group = 4
+    group = 8
     groups = expert_count // group
     within = (jnp.arange(expert_count, dtype=jnp.int32) % group * tok_rows)[:, None, None]
     column = jnp.where(owner >= 0, owner + within, -1)

time: 245 us -> 246 us (level)
  no operation moved by 1% of the time
where the time goes in v9:
time: 246 us
  waiting for transfers between devices  139 us (57%)
  matrix products  36.8 us (15%)
  local copies, waits for them, and re-layouts  20.2 us (8%)
  Pallas kernels  15.9 us (6%)
  starting transfers between devices  14.4 us (6%)
  between operations  14.3 us (6%)
  other arithmetic  5.11 us (2%)
    reduce_scatter x1, waiting for transfers between devices, per_device(): lax.psum_scatter(jnp.einsum('esd,esf->def', grad_slots, weighted, preferr...  71.6 us
    all_gather x1, waiting for transfers between devices, per_device(): gathered = lax.all_gather(grad_out, 'expert')  50.7 us
    dot_general x1, matrix products, per_device(): jnp.einsum('esd,def->esf', grad_slots, down_weight, preferred_element_typ...  20 us
    dot_general x1, matrix products, per_device(): jnp.einsum('esd,esf->def', grad_slots, weighted, preferred_element_type=j...  16.8 us
    pallas_call x1, Pallas kernels, pick(): pl.pallas_call(pick_kernel, out_shape=jax.ShapeDtypeStruct((local, groups...  15.9 us
    all_to_all x1, starting transfers between devices, per_device(): lax.all_to_all(info, 'expert', split_axis=0, concat_axis=0, tiled=True)  9.43 us
    all_to_all x1, waiting for transfers between devices, per_device(): lax.all_to_all(info, 'expert', split_axis=0, concat_axis=0, tiled=True)  8.71 us
    unnamed x5, local copies, waits for them, and re-layouts  7.38 us
  transfers between devices with their start and end apart: 4, of which 4 were waited for; matrix products, arithmetic and copies ran while one was open for 16% of the time, Pallas kernels for 0%

profile of v9, /device:TPU:1, one launch (start us, length us, event | category | flops | bytes accessed | tf_op | source)
XLA Modules:
  0.0 245.7 jit_solution(11027947792361147672)
XLA Ops:
  7.2 0.7 all-gather.3.cloned.1.call-update
  7.9 0.7 convert_element_type.36
  8.6 0.7 convert_element_type.37
  9.3 0.1 copy.66
  9.5 0.8 broadcast_in_dim.51
  10.3 9.4 %all-to-all-start = ((f32[32,1,2048]{2,1,0:T(1,128)}), f32[32,1,2048]{2,1,0:T(1,128)S(1)}, u32[]{:S(2)}, u32[]{:S(2)}) async-start(f32[32,1,2048]{2,1,0:T(1,128)} %broadcast_in_dim.51), calls=%async_computation | async-start | bytes 524288 | tf_op jit(solution)/shard_map/all_to_all | solution.py:68
  19.8 0.1 eq.67
  19.9 8.7 %all-to-all-done = f32[32,1,2048]{2,1,0:T(1,128)S(1)} async-done(((f32[32,1,2048]{2,1,0:T(1,128)}), f32[32,1,2048]{2,1,0:T(1,128)S(1)}, u32[]{:S(2)}, u32[]{:S(2)}) %all-to-all-start) | async-done | bytes 262176 | tf_op jit(solution)/shard_map/all_to_all | solution.py:68
  28.7 0.3 copy.67
  29.1 0.2 copy.68
  29.2 0.1 eq.64
  29.4 0.2 eq.65
  29.6 0.1 convert_bitcast_fusion.1
  29.7 0.2 copy.69
  29.9 0.3 fusion.11
  30.3 0.1 copy.71
  30.4 0.2 copy.72
  30.7 0.1 eq.70
  30.9 0.3 copy.73
  31.2 0.2 copy.74
  31.4 1.1 select_reduce_fusion.1
  32.5 0.1 copy.75
  32.6 0.1 mul.50
  32.7 1.5 select_reduce_fusion
  34.2 0.1 copy.76
  34.4 1.5 reshape.141.column_ref
  35.8 50.7 %all-gather.3.cloned.1.call-done = bf16[4096,2048]{1,0:T(8,128)(2,1)} async-done(((bf16[128,2048]{1,0:T(8,128)(2,1)}), bf16[4096,2048]{1,0:T(8,128)(2,1)}) %all-gather.3.cloned.1.call-update) | async-done | bytes 16777232 | tf_op jit(solution)/shard_map/all_gather | solution.py:72
  86.5 15.9 %shard_map.76 = bf16[4,4,160,2048]{3,2,1,0:T(8,128)(2,1)} custom-call(s32[4,640,1]{2,1,0:T(8,128)} %reshape.141.column_ref, bf16[32,128,2048]{2,1,0:T(8,128)(2,1)} %bitcast.67), custom_call_target="tpu_custom_call" | custom-call | flops 10737418240 | bytes 27262976 | tf_op jit(solution)/shard_map/pallas_call | solution.py:26
  102.4 16.8 %convert_bitcast_fusion = bf16[2048,4,768]{0,2,1:T(8,128)(2,1)} fusion(bf16[4,640,2048]{2,1,0:T(8,128)(2,1)} %bitcast.68, bf16[4,1,640,768]{3,2,1,0:T(8,128)(2,1)} %param.8, f32[4,640]{1,0:T(4,128)S(1)} %mul.50), kind=kOutput, calls=%fused_computation.3 | convolution fusion | flops 8065253376 | bytes 27011072 | tf_op jit(solution)/shard_map/esd,esf->def/dot_general | solution.py:102
  119.2 0.7 copy-done
  119.9 0.1 copy.82
  120.0 0.1 eq.78
  120.1 0.1 eq.74
  120.2 0.1 copy.88
  120.3 0.2 fusion.13
  120.6 0.1 copy.89
  120.7 0.2 copy.90
  121.1 0.1 reshape.132
  121.2 20.0 %fusion.3 = (f32[4,640]{1,0:T(4,128)S(1)}, bf16[4,1,640,768]{3,2,1,0:T(8,128)(2,1)}) fusion(bf16[4,1,640,768]{3,2,1,0:T(8,128)(2,1)} %param.8, f32[4,640]{1,0:T(4,128)S(1)} %mul.50, bf16[4,640,2048]{2,1,0:T(8,128)(2,1)} %bitcast.69, bf16[2048,4,768]{2,1,0:T(4,128)(2,1)} %param.9), kind=kOutput, calls=%fused_computation.10 | convolution fusion | flops 8062891520 | bytes 30953472 | tf_op jit(solution)/shard_map/esd,def->esf/dot_general | solution.py:109
  141.2 0.1 reshape.127
  141.3 0.7 copy.91
  142.0 4.9 %all-to-all-start.1 = ((f32[4,32,20]{2,0,1:T(4,128)}), f32[4,32,20]{2,0,1:T(4,128)S(1)}, u32[]{:S(2)}, u32[]{:S(2)}) async-start(f32[4,32,20]{2,0,1:T(4,128)} %copy.91), calls=%async_computation.2 | async-start | bytes 131072 | tf_op jit(solution)/shard_map/all_to_all | solution.py:114
  147.0 7.3 %all-to-all-done.1 = f32[4,32,20]{2,0,1:T(4,128)S(1)} async-done(((f32[4,32,20]{2,0,1:T(4,128)}), f32[4,32,20]{2,0,1:T(4,128)S(1)}, u32[]{:S(2)}, u32[]{:S(2)}) %all-to-all-start.1) | async-done | bytes 10272 | tf_op jit(solution)/shard_map/all_to_all | solution.py:114
  154.3 0.1 reshape.128
  154.4 6.2 %gather_fusion = f32[1024]{0:T(1024)S(1)} fusion(f32[2560]{0:T(1024)S(1)} %reshape.128, s32[1024]{0:T(1024)S(1)} %broadcast_clamp_fusion), kind=kCustom, calls=%fused_computation | custom fusion | bytes 12288 | tf_op jit(solution)/shard_map/jit(_take)/gather | solution.py:121
  160.6 0.7 copy.95
  161.3 71.6 %reduce-scatter.2.cloned.1.call-done = bf16[512,4,768]{0,2,1:T(8,128)(2,1)} async-done(((bf16[2048,4,768]{0,2,1:T(8,128)(2,1)}), bf16[512,4,768]{0,2,1:T(8,128)(2,1)}) %reduce-scatter.2.cloned.1.call-update) | async-done | bytes 3145744 | tf_op jit(solution)/shard_map/reduce_scatter | solution.py:101
  232.9 6.0 %copy.94 = bf16[512,4,768]{2,1,0:T(4,128)(2,1)} copy(bf16[512,4,768]{0,2,1:T(8,128)(2,1)} %reduce-scatter.2.cloned.1.call-done) | data formatting | bytes 6291456
  (31 shorter events, 0.9 us)
Async XLA Ops:
  7.2 79.4 %all-gather.3.cloned.1.call-start = ((), (), s32[]{:S(2)}) async-start(), calls=%async_computation.4 | async-start | bytes 17301504 | tf_op jit(solution)/shard_map/all_gather | solution.py:72
  10.3 18.4 %all-to-all-start = ((f32[32,1,2048]{2,1,0:T(1,128)}), f32[32,1,2048]{2,1,0:T(1,128)S(1)}, u32[]{:S(2)}, u32[]{:S(2)}) async-start(f32[32,1,2048]{2,1,0:T(1,128)} %broadcast_in_dim.51), calls=%async_computation | async-start | bytes 524288 | tf_op jit(solution)/shard_map/all_to_all | solution.py:68
  19.7 213.2 %reduce-scatter.2.cloned.1.call-start = ((), (), s32[]{:S(2)}) async-start(), calls=%async_computation.3 | async-start | bytes 15728640 | tf_op jit(solution)/shard_map/reduce_scatter | solution.py:101
  119.2 0.7 copy-start
  142.0 12.3 %all-to-all-start.1 = ((f32[4,32,20]{2,0,1:T(4,128)}), f32[4,32,20]{2,0,1:T(4,128)S(1)}, u32[]{:S(2)}, u32[]{:S(2)}) async-start(f32[4,32,20]{2,0,1:T(4,128)} %copy.91), calls=%async_computation.2 | async-start | bytes 131072 | tf_op jit(solution)/shard_map/all_to_all | solution.py:114
Sparse Core Ops, SparseCore 0:
  10.3 76.2 all-gather.2
  119.3 113.5 reduce-scatter.1

commit v10 on v5

--- a/solution.py
+++ b/solution.py
@@ -23,15 +23,16 @@
     sources, tok, _ = gathered.shape
     group = sources // groups
     block = rows_per // local
+    span = 512
     return pl.pallas_call(
         pick_kernel,
         out_shape=jax.ShapeDtypeStruct((local, groups, block, width), gathered.dtype),
-        grid=(groups,),
+        grid=(groups, width // span),
         in_specs=[
-            pl.BlockSpec((1, rows_per, 1), lambda g: (g, 0, 0)),
-            pl.BlockSpec((group, tok, width), lambda g: (g, 0, 0)),
+            pl.BlockSpec((1, rows_per, 1), lambda g, n: (g, 0, 0)),
+            pl.BlockSpec((group, tok, span), lambda g, n: (g, 0, n)),
         ],
-        out_specs=pl.BlockSpec((local, 1, block, width), lambda g: (0, g, 0, 0)),
+        out_specs=pl.BlockSpec((local, 1, block, span), lambda g, n: (0, g, 0, n)),
         cost_estimate=pl.CostEstimate(
             flops=2 * groups * rows_per * group * tok * width,
             bytes_accessed=sources * tok * width * 2 + groups * rows_per * width * 2,

time: 245 us -> 258 us (1.053)
  Pallas kernels: 15.1 us -> 27.1 us
    pallas_call x1, Pallas kernels: 15.1 us -> 27.1 us  [pick(): pl.pallas_call(pick_kernel, out_shape=jax.ShapeDtypeStruct((local, groups...]
  transfers between devices with their start and end apart: 4 -> 4, of which waited for: 4 -> 4; matrix products, arithmetic and copies ran while one was open for 16% -> 15% of each run, Pallas kernels for 0% -> 0%
where the time goes in v10:
time: 258 us; the launch traced here: 257 us
  waiting for transfers between devices  139 us (54%)
  matrix products  36.3 us (14%)
  Pallas kernels  27.1 us (11%)
  local copies, waits for them, and re-layouts  20.2 us (8%)
  starting transfers between devices  14.6 us (6%)
  between operations  14.3 us (6%)
  other arithmetic  5.12 us (2%)
    reduce_scatter x1, waiting for transfers between devices, per_device(): lax.psum_scatter(jnp.einsum('esd,esf->def', grad_slots, weighted, preferr...  71.8 us
    all_gather x1, waiting for transfers between devices, per_device(): gathered = lax.all_gather(grad_out, 'expert')  50.7 us
    pallas_call x1, Pallas kernels, pick(): pl.pallas_call(pick_kernel, out_shape=jax.ShapeDtypeStruct((local, groups...  27.1 us
    dot_general x1, matrix products, per_device(): jnp.einsum('esd,def->esf', grad_slots, down_weight, preferred_element_typ...  19.5 us
    dot_general x1, matrix products, per_device(): jnp.einsum('esd,esf->def', grad_slots, weighted, preferred_element_type=j...  16.8 us
    all_to_all x1, starting transfers between devices, per_device(): lax.all_to_all(info, 'expert', split_axis=0, concat_axis=0, tiled=True)  9.43 us
    all_to_all x1, waiting for transfers between devices, per_device(): lax.all_to_all(info, 'expert', split_axis=0, concat_axis=0, tiled=True)  8.71 us
    unnamed x5, local copies, waits for them, and re-layouts  7.38 us
  transfers between devices with their start and end apart: 4, of which 4 were waited for; matrix products, arithmetic and copies ran while one was open for 15% of the time, Pallas kernels for 0%

profile of v10, /device:TPU:1, one launch (start us, length us, event | category | flops | bytes accessed | tf_op | source)
XLA Modules:
  0.0 257.0 jit_solution(4864478121023680864)
XLA Ops:
  7.2 0.7 all-gather.3.cloned.1.call-update
  7.9 0.7 convert_element_type.36
  8.6 0.7 convert_element_type.37
  9.3 0.1 copy.66
  9.5 0.8 broadcast_in_dim.51
  10.3 9.4 %all-to-all-start = ((f32[32,1,2048]{2,1,0:T(1,128)}), f32[32,1,2048]{2,1,0:T(1,128)S(1)}, u32[]{:S(2)}, u32[]{:S(2)}) async-start(f32[32,1,2048]{2,1,0:T(1,128)} %broadcast_in_dim.51), calls=%async_computation | async-start | bytes 524288 | tf_op jit(solution)/shard_map/all_to_all | solution.py:69
  19.8 0.1 eq.67
  19.9 8.7 %all-to-all-done = f32[32,1,2048]{2,1,0:T(1,128)S(1)} async-done(((f32[32,1,2048]{2,1,0:T(1,128)}), f32[32,1,2048]{2,1,0:T(1,128)S(1)}, u32[]{:S(2)}, u32[]{:S(2)}) %all-to-all-start) | async-done | bytes 262176 | tf_op jit(solution)/shard_map/all_to_all | solution.py:69
  28.7 0.3 copy.67
  29.1 0.2 copy.68
  29.2 0.1 eq.64
  29.4 0.2 eq.65
  29.6 0.1 convert_bitcast_fusion.1
  29.7 0.2 copy.69
  29.9 0.3 fusion.11
  30.3 0.1 copy.71
  30.4 0.2 copy.72
  30.7 0.1 eq.70
  30.9 0.3 copy.73
  31.2 0.2 copy.74
  31.4 1.1 select_reduce_fusion.1
  32.5 0.1 copy.75
  32.6 0.1 mul.50
  32.7 1.5 select_reduce_fusion
  34.2 0.1 copy.76
  34.4 1.5 reshape.141.column_ref
  35.9 50.7 %all-gather.3.cloned.1.call-done = bf16[4096,2048]{1,0:T(8,128)(2,1)} async-done(((bf16[128,2048]{1,0:T(8,128)(2,1)}), bf16[4096,2048]{1,0:T(8,128)(2,1)}) %all-gather.3.cloned.1.call-update) | async-done | bytes 16777232 | tf_op jit(solution)/shard_map/all_gather | solution.py:73
  86.5 27.1 %shard_map.76 = bf16[4,8,80,2048]{3,2,1,0:T(8,128)(2,1)} custom-call(s32[8,320,1]{2,1,0:T(8,128)} %reshape.141.column_ref, bf16[32,128,2048]{2,1,0:T(8,128)(2,1)} %bitcast.51), custom_call_target="tpu_custom_call" | custom-call | flops 5368709120 | bytes 27262976 | tf_op jit(solution)/shard_map/pallas_call | solution.py:27
  113.7 16.8 %convert_bitcast_fusion = bf16[2048,4,768]{0,2,1:T(8,128)(2,1)} fusion(bf16[4,640,2048]{2,1,0:T(8,128)(2,1)} %bitcast.52, bf16[4,1,640,768]{3,2,1,0:T(8,128)(2,1)} %param.8, f32[4,640]{1,0:T(4,128)S(1)} %mul.50), kind=kOutput, calls=%fused_computation.3 | convolution fusion | flops 8065253376 | bytes 27011072 | tf_op jit(solution)/shard_map/esd,esf->def/dot_general | solution.py:103
  130.5 0.7 copy-done
  131.1 0.1 copy.82
  131.2 0.1 eq.78
  131.3 0.1 eq.74
  131.4 0.1 copy.88
  131.5 0.2 fusion.13
  131.8 0.1 copy.89
  131.9 0.2 copy.90
  132.4 0.1 reshape.132
  132.5 19.5 %fusion.3 = (f32[4,640]{1,0:T(4,128)S(1)}, bf16[4,1,640,768]{3,2,1,0:T(8,128)(2,1)}) fusion(bf16[4,1,640,768]{3,2,1,0:T(8,128)(2,1)} %param.8, f32[4,640]{1,0:T(4,128)S(1)} %mul.50, bf16[4,640,2048]{2,1,0:T(8,128)(2,1)} %bitcast.53, bf16[2048,4,768]{2,1,0:T(4,128)(2,1)} %param.9), kind=kOutput, calls=%fused_computation.10 | convolution fusion | flops 8062891520 | bytes 30953472 | tf_op jit(solution)/shard_map/esd,def->esf/dot_general | solution.py:110
  152.0 0.1 reshape.127
  152.1 0.7 copy.91
  152.8 5.1 %all-to-all-start.1 = ((f32[4,32,20]{2,0,1:T(4,128)}), f32[4,32,20]{2,0,1:T(4,128)S(1)}, u32[]{:S(2)}, u32[]{:S(2)}) async-start(f32[4,32,20]{2,0,1:T(4,128)} %copy.91), calls=%async_computation.2 | async-start | bytes 131072 | tf_op jit(solution)/shard_map/all_to_all | solution.py:115
  158.0 7.3 %all-to-all-done.1 = f32[4,32,20]{2,0,1:T(4,128)S(1)} async-done(((f32[4,32,20]{2,0,1:T(4,128)}), f32[4,32,20]{2,0,1:T(4,128)S(1)}, u32[]{:S(2)}, u32[]{:S(2)}) %all-to-all-start.1) | async-done | bytes 10272 | tf_op jit(solution)/shard_map/all_to_all | solution.py:115
  165.3 0.1 reshape.128
  165.4 6.2 %gather_fusion = f32[1024]{0:T(1024)S(1)} fusion(f32[2560]{0:T(1024)S(1)} %reshape.128, s32[1024]{0:T(1024)S(1)} %broadcast_clamp_fusion), kind=kCustom, calls=%fused_computation | custom fusion | bytes 12288 | tf_op jit(solution)/shard_map/jit(_take)/gather | solution.py:122
  171.7 0.7 copy.95
  172.3 71.8 %reduce-scatter.2.cloned.1.call-done = bf16[512,4,768]{0,2,1:T(8,128)(2,1)} async-done(((bf16[2048,4,768]{0,2,1:T(8,128)(2,1)}), bf16[512,4,768]{0,2,1:T(8,128)(2,1)}) %reduce-scatter.2.cloned.1.call-update) | async-done | bytes 3145744 | tf_op jit(solution)/shard_map/reduce_scatter | solution.py:102
  244.2 6.0 %copy.94 = bf16[512,4,768]{2,1,0:T(4,128)(2,1)} copy(bf16[512,4,768]{0,2,1:T(8,128)(2,1)} %reduce-scatter.2.cloned.1.call-done) | data formatting | bytes 6291456
  (31 shorter events, 0.9 us)
Async XLA Ops:
  7.2 79.4 %all-gather.3.cloned.1.call-start = ((), (), s32[]{:S(2)}) async-start(), calls=%async_computation.4 | async-start | bytes 17301504 | tf_op jit(solution)/shard_map/all_gather | solution.py:73
  10.3 18.4 %all-to-all-start = ((f32[32,1,2048]{2,1,0:T(1,128)}), f32[32,1,2048]{2,1,0:T(1,128)S(1)}, u32[]{:S(2)}, u32[]{:S(2)}) async-start(f32[32,1,2048]{2,1,0:T(1,128)} %broadcast_in_dim.51), calls=%async_computation | async-start | bytes 524288 | tf_op jit(solution)/shard_map/all_to_all | solution.py:69
  19.7 224.4 %reduce-scatter.2.cloned.1.call-start = ((), (), s32[]{:S(2)}) async-start(), calls=%async_computation.3 | async-start | bytes 15728640 | tf_op jit(solution)/shard_map/reduce_scatter | solution.py:102
  130.4 0.7 copy-start
  152.8 12.5 %all-to-all-start.1 = ((f32[4,32,20]{2,0,1:T(4,128)}), f32[4,32,20]{2,0,1:T(4,128)S(1)}, u32[]{:S(2)}, u32[]{:S(2)}) async-start(f32[4,32,20]{2,0,1:T(4,128)} %copy.91), calls=%async_computation.2 | async-start | bytes 131072 | tf_op jit(solution)/shard_map/all_to_all | solution.py:115
Sparse Core Ops, SparseCore 0:
  10.3 76.2 all-gather.2
  130.6 113.5 reduce-scatter.1

commit v11 on v5

--- a/solution.py
+++ b/solution.py
@@ -6,16 +6,19 @@
 
 
 def pick_kernel(column_ref, rows_ref, out_ref):
-    column = column_ref[0]
-    local, _, block, width = out_ref.shape
-    group, tok, _ = rows_ref.shape
-    onehot = (
-        column == lax.broadcasted_iota(jnp.int32, (column.shape[0], group * tok), 1)
-    ).astype(rows_ref.dtype)
-    rows = rows_ref[...].reshape(group * tok, width)
-    result = jnp.dot(onehot, rows, preferred_element_type=jnp.float32).astype(out_ref.dtype)
-    for j in range(local):
-        out_ref[j, 0] = result[j * block:(j + 1) * block]
+    local, steps, block, width = out_ref.shape
+    rows_per = column_ref.shape[1]
+    group = rows_ref.shape[0] // steps
+    tok = rows_ref.shape[1]
+    for h in range(steps):
+        column = column_ref[h]
+        onehot = (
+            column == lax.broadcasted_iota(jnp.int32, (rows_per, group * tok), 1)
+        ).astype(rows_ref.dtype)
+        rows = rows_ref[h * group:(h + 1) * group].reshape(group * tok, width)
+        result = jnp.dot(onehot, rows, preferred_element_type=jnp.float32).astype(out_ref.dtype)
+        for j in range(local):
+            out_ref[j, h] = result[j * block:(j + 1) * block]
 
 
 def pick(column, gathered, width, local):
@@ -23,15 +26,16 @@
     sources, tok, _ = gathered.shape
     group = sources // groups
     block = rows_per // local
+    steps = 2
     return pl.pallas_call(
         pick_kernel,
         out_shape=jax.ShapeDtypeStruct((local, groups, block, width), gathered.dtype),
-        grid=(groups,),
+        grid=(groups // steps,),
         in_specs=[
-            pl.BlockSpec((1, rows_per, 1), lambda g: (g, 0, 0)),
-            pl.BlockSpec((group, tok, width), lambda g: (g, 0, 0)),
+            pl.BlockSpec((steps, rows_per, 1), lambda g: (g, 0, 0)),
+            pl.BlockSpec((steps * group, tok, width), lambda g: (g, 0, 0)),
         ],
-        out_specs=pl.BlockSpec((local, 1, block, width), lambda g: (0, g, 0, 0)),
+        out_specs=pl.BlockSpec((local, steps, block, width), lambda g: (0, g, 0, 0)),
         cost_estimate=pl.CostEstimate(
             flops=2 * groups * rows_per * group * tok * width,
             bytes_accessed=sources * tok * width * 2 + groups * rows_per * width * 2,

time: 245 us -> 243 us (level)
  no operation moved by 1% of the time
where the time goes in v11:
time: 243 us
  waiting for transfers between devices  139 us (57%)
  matrix products  36.8 us (15%)
  local copies, waits for them, and re-layouts  20.2 us (8%)
  starting transfers between devices  14.4 us (6%)
  between operations  14.3 us (6%)
  Pallas kernels  12.8 us (5%)
  other arithmetic  5.12 us (2%)
    reduce_scatter x1, waiting for transfers between devices, per_device(): lax.psum_scatter(jnp.einsum('esd,esf->def', grad_slots, weighted, preferr...  71.6 us
    all_gather x1, waiting for transfers between devices, per_device(): gathered = lax.all_gather(grad_out, 'expert')  50.7 us
    dot_general x1, matrix products, per_device(): jnp.einsum('esd,def->esf', grad_slots, down_weight, preferred_element_typ...  20 us
    dot_general x1, matrix products, per_device(): jnp.einsum('esd,esf->def', grad_slots, weighted, preferred_element_type=j...  16.8 us
    pallas_call x1, Pallas kernels, pick(): pl.pallas_call(pick_kernel, out_shape=jax.ShapeDtypeStruct((local, groups...  12.8 us
    all_to_all x1, starting transfers between devices, per_device(): lax.all_to_all(info, 'expert', split_axis=0, concat_axis=0, tiled=True)  9.43 us
    all_to_all x1, waiting for transfers between devices, per_device(): lax.all_to_all(info, 'expert', split_axis=0, concat_axis=0, tiled=True)  8.71 us
    unnamed x5, local copies, waits for them, and re-layouts  7.38 us
  transfers between devices with their start and end apart: 4, of which 4 were waited for; matrix products, arithmetic and copies ran while one was open for 16% of the time, Pallas kernels for 0%

profile of v11, /device:TPU:1, one launch (start us, length us, event | category | flops | bytes accessed | tf_op | source)
XLA Modules:
  0.0 242.6 jit_solution(1596521296956665770)
XLA Ops:
  7.2 0.7 all-gather.3.cloned.1.call-update
  7.9 0.7 convert_element_type.36
  8.6 0.7 convert_element_type.37
  9.3 0.1 copy.66
  9.5 0.8 broadcast_in_dim.51
  10.3 9.4 %all-to-all-start = ((f32[32,1,2048]{2,1,0:T(1,128)}), f32[32,1,2048]{2,1,0:T(1,128)S(1)}, u32[]{:S(2)}, u32[]{:S(2)}) async-start(f32[32,1,2048]{2,1,0:T(1,128)} %broadcast_in_dim.51), calls=%async_computation | async-start | bytes 524288 | tf_op jit(solution)/shard_map/all_to_all | solution.py:72
  19.8 0.1 eq.67
  19.9 8.7 %all-to-all-done = f32[32,1,2048]{2,1,0:T(1,128)S(1)} async-done(((f32[32,1,2048]{2,1,0:T(1,128)}), f32[32,1,2048]{2,1,0:T(1,128)S(1)}, u32[]{:S(2)}, u32[]{:S(2)}) %all-to-all-start) | async-done | bytes 262176 | tf_op jit(solution)/shard_map/all_to_all | solution.py:72
  28.7 0.3 copy.67
  29.1 0.2 copy.68
  29.2 0.1 eq.64
  29.4 0.2 eq.65
  29.6 0.1 convert_bitcast_fusion.1
  29.7 0.2 copy.69
  29.9 0.3 fusion.11
  30.3 0.1 copy.71
  30.4 0.2 copy.72
  30.7 0.1 eq.70
  30.9 0.3 copy.73
  31.2 0.2 copy.74
  31.4 1.1 select_reduce_fusion.1
  32.5 0.1 copy.75
  32.6 0.1 mul.50
  32.7 1.5 select_reduce_fusion
  34.2 0.1 copy.76
  34.4 1.5 reshape.141.column_ref
  35.9 50.7 %all-gather.3.cloned.1.call-done = bf16[4096,2048]{1,0:T(8,128)(2,1)} async-done(((bf16[128,2048]{1,0:T(8,128)(2,1)}), bf16[4096,2048]{1,0:T(8,128)(2,1)}) %all-gather.3.cloned.1.call-update) | async-done | bytes 16777232 | tf_op jit(solution)/shard_map/all_gather | solution.py:76
  86.5 12.8 %shard_map.76 = bf16[4,8,80,2048]{3,2,1,0:T(8,128)(2,1)} custom-call(s32[8,320,1]{2,1,0:T(8,128)} %reshape.141.column_ref, bf16[32,128,2048]{2,1,0:T(8,128)(2,1)} %bitcast.51), custom_call_target="tpu_custom_call" | custom-call | flops 5368709120 | bytes 27262976 | tf_op jit(solution)/shard_map/pallas_call | solution.py:30
  99.3 16.8 %convert_bitcast_fusion = bf16[2048,4,768]{0,2,1:T(8,128)(2,1)} fusion(bf16[4,640,2048]{2,1,0:T(8,128)(2,1)} %bitcast.52, bf16[4,1,640,768]{3,2,1,0:T(8,128)(2,1)} %param.8, f32[4,640]{1,0:T(4,128)S(1)} %mul.50), kind=kOutput, calls=%fused_computation.3 | convolution fusion | flops 8065253376 | bytes 27011072 | tf_op jit(solution)/shard_map/esd,esf->def/dot_general | solution.py:106
  116.1 0.7 copy-done
  116.8 0.1 copy.82
  116.9 0.1 eq.78
  117.0 0.1 eq.74
  117.1 0.1 copy.88
  117.2 0.2 fusion.13
  117.5 0.1 copy.89
  117.6 0.2 copy.90
  118.0 0.1 reshape.132
  118.1 20.0 %fusion.3 = (f32[4,640]{1,0:T(4,128)S(1)}, bf16[4,1,640,768]{3,2,1,0:T(8,128)(2,1)}) fusion(bf16[4,1,640,768]{3,2,1,0:T(8,128)(2,1)} %param.8, f32[4,640]{1,0:T(4,128)S(1)} %mul.50, bf16[4,640,2048]{2,1,0:T(8,128)(2,1)} %bitcast.53, bf16[2048,4,768]{2,1,0:T(4,128)(2,1)} %param.9), kind=kOutput, calls=%fused_computation.10 | convolution fusion | flops 8062891520 | bytes 30953472 | tf_op jit(solution)/shard_map/esd,def->esf/dot_general | solution.py:113
  138.1 0.1 reshape.127
  138.2 0.7 copy.91
  138.9 4.9 %all-to-all-start.1 = ((f32[4,32,20]{2,0,1:T(4,128)}), f32[4,32,20]{2,0,1:T(4,128)S(1)}, u32[]{:S(2)}, u32[]{:S(2)}) async-start(f32[4,32,20]{2,0,1:T(4,128)} %copy.91), calls=%async_computation.2 | async-start | bytes 131072 | tf_op jit(solution)/shard_map/all_to_all | solution.py:118
  143.8 7.3 %all-to-all-done.1 = f32[4,32,20]{2,0,1:T(4,128)S(1)} async-done(((f32[4,32,20]{2,0,1:T(4,128)}), f32[4,32,20]{2,0,1:T(4,128)S(1)}, u32[]{:S(2)}, u32[]{:S(2)}) %all-to-all-start.1) | async-done | bytes 10272 | tf_op jit(solution)/shard_map/all_to_all | solution.py:118
  151.2 0.1 reshape.128
  151.3 6.2 %gather_fusion = f32[1024]{0:T(1024)S(1)} fusion(f32[2560]{0:T(1024)S(1)} %reshape.128, s32[1024]{0:T(1024)S(1)} %broadcast_clamp_fusion), kind=kCustom, calls=%fused_computation | custom fusion | bytes 12288 | tf_op jit(solution)/shard_map/jit(_take)/gather | solution.py:125
  157.5 0.7 copy.95
  158.2 71.6 %reduce-scatter.2.cloned.1.call-done = bf16[512,4,768]{0,2,1:T(8,128)(2,1)} async-done(((bf16[2048,4,768]{0,2,1:T(8,128)(2,1)}), bf16[512,4,768]{0,2,1:T(8,128)(2,1)}) %reduce-scatter.2.cloned.1.call-update) | async-done | bytes 3145744 | tf_op jit(solution)/shard_map/reduce_scatter | solution.py:105
  229.8 6.0 %copy.94 = bf16[512,4,768]{2,1,0:T(4,128)(2,1)} copy(bf16[512,4,768]{0,2,1:T(8,128)(2,1)} %reduce-scatter.2.cloned.1.call-done) | data formatting | bytes 6291456
  (31 shorter events, 0.9 us)
Async XLA Ops:
  7.2 79.4 %all-gather.3.cloned.1.call-start = ((), (), s32[]{:S(2)}) async-start(), calls=%async_computation.4 | async-start | bytes 17301504 | tf_op jit(solution)/shard_map/all_gather | solution.py:76
  10.3 18.4 %all-to-all-start = ((f32[32,1,2048]{2,1,0:T(1,128)}), f32[32,1,2048]{2,1,0:T(1,128)S(1)}, u32[]{:S(2)}, u32[]{:S(2)}) async-start(f32[32,1,2048]{2,1,0:T(1,128)} %broadcast_in_dim.51), calls=%async_computation | async-start | bytes 524288 | tf_op jit(solution)/shard_map/all_to_all | solution.py:72
  19.7 210.1 %reduce-scatter.2.cloned.1.call-start = ((), (), s32[]{:S(2)}) async-start(), calls=%async_computation.3 | async-start | bytes 15728640 | tf_op jit(solution)/shard_map/reduce_scatter | solution.py:105
  116.1 0.7 copy-start
  138.9 12.3 %all-to-all-start.1 = ((f32[4,32,20]{2,0,1:T(4,128)}), f32[4,32,20]{2,0,1:T(4,128)S(1)}, u32[]{:S(2)}, u32[]{:S(2)}) async-start(f32[4,32,20]{2,0,1:T(4,128)} %copy.91), calls=%async_computation.2 | async-start | bytes 131072 | tf_op jit(solution)/shard_map/all_to_all | solution.py:118
Sparse Core Ops, SparseCore 0:
  10.3 76.2 all-gather.2
  116.2 113.5 reduce-scatter.1

commit v12 on v11

--- a/solution.py
+++ b/solution.py
@@ -26,7 +26,7 @@
     sources, tok, _ = gathered.shape
     group = sources // groups
     block = rows_per // local
-    steps = 2
+    steps = 4
     return pl.pallas_call(
         pick_kernel,
         out_shape=jax.ShapeDtypeStruct((local, groups, block, width), gathered.dtype),

time: 243 us -> 242 us (level)
  no operation moved by 1% of the time
where the time goes in v12:
time: 242 us
  waiting for transfers between devices  139 us (57%)
  matrix products  36.7 us (15%)
  local copies, waits for them, and re-layouts  20.2 us (8%)
  starting transfers between devices  14.5 us (6%)
  between operations  14.3 us (6%)
  Pallas kernels  11.9 us (5%)
  other arithmetic  5.12 us (2%)
    reduce_scatter x1, waiting for transfers between devices, per_device(): lax.psum_scatter(jnp.einsum('esd,esf->def', grad_slots, weighted, preferr...  71.6 us
    all_gather x1, waiting for transfers between devices, per_device(): gathered = lax.all_gather(grad_out, 'expert')  50.7 us
    dot_general x1, matrix products, per_device(): jnp.einsum('esd,def->esf', grad_slots, down_weight, preferred_element_typ...  20 us
    dot_general x1, matrix products, per_device(): jnp.einsum('esd,esf->def', grad_slots, weighted, preferred_element_type=j...  16.8 us
    pallas_call x1, Pallas kernels, pick(): pl.pallas_call(pick_kernel, out_shape=jax.ShapeDtypeStruct((local, groups...  11.9 us
    all_to_all x1, starting transfers between devices, per_device(): lax.all_to_all(info, 'expert', split_axis=0, concat_axis=0, tiled=True)  9.43 us
    all_to_all x1, waiting for transfers between devices, per_device(): lax.all_to_all(info, 'expert', split_axis=0, concat_axis=0, tiled=True)  8.71 us
    unnamed x5, local copies, waits for them, and re-layouts  7.38 us
  transfers between devices with their start and end apart: 4, of which 4 were waited for; matrix products, arithmetic and copies ran while one was open for 16% of the time, Pallas kernels for 0%

profile of v12, /device:TPU:1, one launch (start us, length us, event | category | flops | bytes accessed | tf_op | source)
XLA Modules:
  0.0 241.7 jit_solution(5516688635989774770)
XLA Ops:
  7.2 0.7 all-gather.3.cloned.1.call-update
  7.9 0.7 convert_element_type.36
  8.6 0.7 convert_element_type.37
  9.3 0.1 copy.66
  9.5 0.8 broadcast_in_dim.51
  10.3 9.4 %all-to-all-start = ((f32[32,1,2048]{2,1,0:T(1,128)}), f32[32,1,2048]{2,1,0:T(1,128)S(1)}, u32[]{:S(2)}, u32[]{:S(2)}) async-start(f32[32,1,2048]{2,1,0:T(1,128)} %broadcast_in_dim.51), calls=%async_computation | async-start | bytes 524288 | tf_op jit(solution)/shard_map/all_to_all | solution.py:72
  19.8 0.1 eq.67
  19.9 8.7 %all-to-all-done = f32[32,1,2048]{2,1,0:T(1,128)S(1)} async-done(((f32[32,1,2048]{2,1,0:T(1,128)}), f32[32,1,2048]{2,1,0:T(1,128)S(1)}, u32[]{:S(2)}, u32[]{:S(2)}) %all-to-all-start) | async-done | bytes 262176 | tf_op jit(solution)/shard_map/all_to_all | solution.py:72
  28.7 0.3 copy.67
  29.1 0.2 copy.68
  29.2 0.1 eq.64
  29.4 0.2 eq.65
  29.6 0.1 convert_bitcast_fusion.1
  29.7 0.2 copy.69
  29.9 0.3 fusion.11
  30.3 0.1 copy.71
  30.4 0.2 copy.72
  30.7 0.1 eq.70
  30.9 0.3 copy.73
  31.2 0.2 copy.74
  31.4 1.1 select_reduce_fusion.1
  32.5 0.1 copy.75
  32.6 0.1 mul.50
  32.7 1.5 select_reduce_fusion
  34.2 0.1 copy.76
  34.4 1.5 reshape.141.column_ref
  35.9 50.7 %all-gather.3.cloned.1.call-done = bf16[4096,2048]{1,0:T(8,128)(2,1)} async-done(((bf16[128,2048]{1,0:T(8,128)(2,1)}), bf16[4096,2048]{1,0:T(8,128)(2,1)}) %all-gather.3.cloned.1.call-update) | async-done | bytes 16777232 | tf_op jit(solution)/shard_map/all_gather | solution.py:76
  86.5 11.9 %shard_map.76 = bf16[4,8,80,2048]{3,2,1,0:T(8,128)(2,1)} custom-call(s32[8,320,1]{2,1,0:T(8,128)} %reshape.141.column_ref, bf16[32,128,2048]{2,1,0:T(8,128)(2,1)} %bitcast.51), custom_call_target="tpu_custom_call" | custom-call | flops 5368709120 | bytes 27262976 | tf_op jit(solution)/shard_map/pallas_call | solution.py:30
  98.4 16.8 %convert_bitcast_fusion = bf16[2048,4,768]{0,2,1:T(8,128)(2,1)} fusion(bf16[4,640,2048]{2,1,0:T(8,128)(2,1)} %bitcast.52, bf16[4,1,640,768]{3,2,1,0:T(8,128)(2,1)} %param.8, f32[4,640]{1,0:T(4,128)S(1)} %mul.50), kind=kOutput, calls=%fused_computation.3 | convolution fusion | flops 8065253376 | bytes 27011072 | tf_op jit(solution)/shard_map/esd,esf->def/dot_general | solution.py:106
  115.2 0.7 copy-done
  115.9 0.1 copy.82
  116.0 0.1 eq.78
  116.1 0.1 eq.74
  116.2 0.1 copy.88
  116.3 0.2 fusion.13
  116.6 0.1 copy.89
  116.7 0.2 copy.90
  117.1 0.1 reshape.132
  117.2 20.0 %fusion.3 = (f32[4,640]{1,0:T(4,128)S(1)}, bf16[4,1,640,768]{3,2,1,0:T(8,128)(2,1)}) fusion(bf16[4,1,640,768]{3,2,1,0:T(8,128)(2,1)} %param.8, f32[4,640]{1,0:T(4,128)S(1)} %mul.50, bf16[4,640,2048]{2,1,0:T(8,128)(2,1)} %bitcast.53, bf16[2048,4,768]{2,1,0:T(4,128)(2,1)} %param.9), kind=kOutput, calls=%fused_computation.10 | convolution fusion | flops 8062891520 | bytes 30953472 | tf_op jit(solution)/shard_map/esd,def->esf/dot_general | solution.py:113
  137.2 0.1 reshape.127
  137.3 0.7 copy.91
  138.0 4.9 %all-to-all-start.1 = ((f32[4,32,20]{2,0,1:T(4,128)}), f32[4,32,20]{2,0,1:T(4,128)S(1)}, u32[]{:S(2)}, u32[]{:S(2)}) async-start(f32[4,32,20]{2,0,1:T(4,128)} %copy.91), calls=%async_computation.2 | async-start | bytes 131072 | tf_op jit(solution)/shard_map/all_to_all | solution.py:118
  143.0 7.3 %all-to-all-done.1 = f32[4,32,20]{2,0,1:T(4,128)S(1)} async-done(((f32[4,32,20]{2,0,1:T(4,128)}), f32[4,32,20]{2,0,1:T(4,128)S(1)}, u32[]{:S(2)}, u32[]{:S(2)}) %all-to-all-start.1) | async-done | bytes 10272 | tf_op jit(solution)/shard_map/all_to_all | solution.py:118
  150.3 0.1 reshape.128
  150.4 6.2 %gather_fusion = f32[1024]{0:T(1024)S(1)} fusion(f32[2560]{0:T(1024)S(1)} %reshape.128, s32[1024]{0:T(1024)S(1)} %broadcast_clamp_fusion), kind=kCustom, calls=%fused_computation | custom fusion | bytes 12288 | tf_op jit(solution)/shard_map/jit(_take)/gather | solution.py:125
  156.7 0.7 copy.95
  157.3 71.6 %reduce-scatter.2.cloned.1.call-done = bf16[512,4,768]{0,2,1:T(8,128)(2,1)} async-done(((bf16[2048,4,768]{0,2,1:T(8,128)(2,1)}), bf16[512,4,768]{0,2,1:T(8,128)(2,1)}) %reduce-scatter.2.cloned.1.call-update) | async-done | bytes 3145744 | tf_op jit(solution)/shard_map/reduce_scatter | solution.py:105
  228.9 6.0 %copy.94 = bf16[512,4,768]{2,1,0:T(4,128)(2,1)} copy(bf16[512,4,768]{0,2,1:T(8,128)(2,1)} %reduce-scatter.2.cloned.1.call-done) | data formatting | bytes 6291456
  (31 shorter events, 0.9 us)
Async XLA Ops:
  7.2 79.4 %all-gather.3.cloned.1.call-start = ((), (), s32[]{:S(2)}) async-start(), calls=%async_computation.4 | async-start | bytes 17301504 | tf_op jit(solution)/shard_map/all_gather | solution.py:76
  10.3 18.4 %all-to-all-start = ((f32[32,1,2048]{2,1,0:T(1,128)}), f32[32,1,2048]{2,1,0:T(1,128)S(1)}, u32[]{:S(2)}, u32[]{:S(2)}) async-start(f32[32,1,2048]{2,1,0:T(1,128)} %broadcast_in_dim.51), calls=%async_computation | async-start | bytes 524288 | tf_op jit(solution)/shard_map/all_to_all | solution.py:72
  19.7 209.2 %reduce-scatter.2.cloned.1.call-start = ((), (), s32[]{:S(2)}) async-start(), calls=%async_computation.3 | async-start | bytes 15728640 | tf_op jit(solution)/shard_map/reduce_scatter | solution.py:105
  115.2 0.7 copy-start
  138.0 12.3 %all-to-all-start.1 = ((f32[4,32,20]{2,0,1:T(4,128)}), f32[4,32,20]{2,0,1:T(4,128)S(1)}, u32[]{:S(2)}, u32[]{:S(2)}) async-start(f32[4,32,20]{2,0,1:T(4,128)} %copy.91), calls=%async_computation.2 | async-start | bytes 131072 | tf_op jit(solution)/shard_map/all_to_all | solution.py:118
Sparse Core Ops, SparseCore 0:
  10.3 76.2 all-gather.2
  115.4 113.5 reduce-scatter.1
